TPU v7x, 1024 devices: a whole 4x8x16 slice. The times are simulated.
1024 devices in a mesh: dp: 16 (over z_lo, core), ctx: 64 (over y, x, z_hi).
Axes of the slice: x: 4, y: 8, z: 16 (z_hi: 2, z_lo: 8; z = z_hi * 8 + z_lo), core: 2. Of those that a mesh axis runs over, the one named last changes fastest.
Arguments:
- queries: bfloat16 [16, 8192, 2048], P('dp', 'ctx'), may hold values from -150 to 150
- key_rows: bfloat16 [16, 8192, 512], P('dp', 'ctx'), may hold values from -5 to 5
- value_rows: bfloat16 [16, 8192, 512], P('dp', 'ctx'), may hold values from -6 to 6
- cotangent: bfloat16 [16, 8192, 2048], P('dp', 'ctx'), may hold values from -6 to 6
- sink_logits: float32 [16], replicated, may hold values from -1 to 3
- run_lengths: int32 [16, 16], P('dp'), may hold values from 1 to 8, 64 in all within a row
- segment_ids: int32 [16, 8192], P('dp', 'ctx'), may hold values from 0 to 15, never falling along the last dimension, each value on 1 to 1024 neighbouring positions
Outputs:
- attended: bfloat16 [16, 8192, 2048], P('dp', 'ctx')
- grad_queries: bfloat16 [16, 8192, 2048], P('dp', 'ctx')
- grad_keys: bfloat16 [16, 8192, 512], P('dp', 'ctx')
- grad_values: bfloat16 [16, 8192, 512], P('dp', 'ctx')
- grad_sink: float32 [16], replicated
Inputs may be any that keep to these rules, and one draw needn't show every extreme that they name: `run_lengths`: in each sequence the trajectories cover all shards in order; each spans 1 to 8 shards and one spans exactly 8. `segment_ids`: never falls along a sequence; each episode spans 1 to 1024 tokens and one spans exactly 1024.
All inputs are finite; a program needn't handle non-finite values.
Results may differ from a plain program's by a relative error of at most 0.04.
Values may be sent and summed in bfloat16 or wider, within the bound.
No kernel may reach another device: no remote copies, remote signals or barrier semaphores. Data moves between devices by JAX's collectives and lax.ppermute only.
A program may use at most 64 MiB of HBM per device.

v0:
```python
import math

import jax
import jax.numpy as jnp
from jax import lax
from jax.experimental import pallas as pl
from jax.experimental.pallas import tpu as pltpu
from jax.sharding import Mesh
from jax.sharding import PartitionSpec as P


HEADS = 16
KV_HEADS = 4
HEAD_DIM = 128
GROUP = HEADS // KV_HEADS
TOK = 128
MOST = 8
KV_COLS = KV_HEADS * HEAD_DIM
PACK_ROWS = 2 * TOK + 8
WIN = MOST * TOK
GROUP_COLS = GROUP * HEAD_DIM
FACTOR = HEAD_DIM ** (-0.5)
CTX = ("ctx_0", "ctx_1", "ctx_2")
DP = ("dp_0", "dp_1")


NT = (((1,), (1,)), ((), ()))
NN = (((1,), (0,)), ((), ()))


def passed_along(array, by):
    devices = lax.axis_size(CTX)
    pairs = [(i, i + by) for i in range(devices) if 0 <= i + by < devices]
    return lax.ppermute(array, CTX, pairs)


def dot(left, right, dims):
    return lax.dot_general(left, right, dims, preferred_element_type=jnp.float32)


def attention_kernel(
    marks_ref,
    sink_ref,
    bias_ref,
    query_ref,
    grad_ref,
    *refs,
):
    packs = refs[:MOST]
    (out_ref, grad_query_ref, near_ref, far2_ref, far4_ref, far6_ref, sink_grad_ref) = refs[
        MOST : MOST + 7
    ]
    mask_ref, score_ref, cross_ref, weight_ref, slope_ref = refs[MOST + 7 :]
    kv_head = pl.program_id(0)

    @pl.when(kv_head == 0)
    def _():
        mask_ref[:TOK, :] = bias_ref[...]
        rows = lax.broadcasted_iota(jnp.int32, (TOK, TOK), 0)
        cols = lax.broadcasted_iota(jnp.int32, (TOK, TOK), 1)
        reach = marks_ref[0]
        first_mark = marks_ref[1].astype(jnp.float32)
        first_count = marks_ref[2]
        for slot in range(1, MOST):
            row = packs[slot][2 * TOK : 2 * TOK + 8, :].astype(jnp.float32)[:1, :]
            same = jnp.sum((row == first_mark).astype(jnp.float32), axis=1, keepdims=True)
            same = jnp.where(slot <= reach, same, 0.0)
            seen = (rows >= TOK - same.astype(jnp.int32)) & (cols < first_count)
            mask_ref[slot * TOK : (slot + 1) * TOK, :] = jnp.where(seen, 0.0, -jnp.inf)

    def stacked(ref):
        return jnp.concatenate(
            [ref[:, g * HEAD_DIM : (g + 1) * HEAD_DIM] for g in range(GROUP)], axis=0
        )

    query = stacked(query_ref)
    grad = stacked(grad_ref)
    keys = jnp.concatenate([pack[:TOK, :] for pack in packs], axis=0)
    values = jnp.concatenate([pack[TOK : 2 * TOK, :] for pack in packs], axis=0)
    score_ref[...] = dot(keys, query, NT)
    cross_ref[...] = dot(values, grad, NT)
    blocks = [slice(slot * TOK, (slot + 1) * TOK) for slot in range(MOST)]
    lanes = [slice(g * TOK, (g + 1) * TOK) for g in range(GROUP)]
    sink_weights = []
    for g in range(GROUP):
        sink = sink_ref[kv_head * GROUP + g]
        best = jnp.full((8, TOK), sink, jnp.float32)
        for rows in blocks:
            scores = score_ref[rows, lanes[g]] * FACTOR + mask_ref[rows, :]
            score_ref[rows, lanes[g]] = scores
            best = jnp.maximum(best, jnp.max(scores.reshape(TOK // 8, 8, TOK), axis=0))
        top = jnp.max(best, axis=0, keepdims=True)
        total = jnp.zeros((8, TOK), jnp.float32)
        for rows in blocks:
            terms = jnp.exp(score_ref[rows, lanes[g]] - top)
            score_ref[rows, lanes[g]] = terms
            total = total + jnp.sum(terms.reshape(TOK // 8, 8, TOK), axis=0)
        sink_exp = jnp.exp(sink - top)
        scale = 1.0 / (jnp.sum(total, axis=0, keepdims=True) + sink_exp)
        for rows in blocks:
            weights = score_ref[rows, lanes[g]] * scale
            score_ref[rows, lanes[g]] = weights
            weight_ref[rows, lanes[g]] = weights.astype(jnp.bfloat16)
        sink_weights.append(sink_exp * scale)
    out_t = dot(values.T, weight_ref[...], NN).astype(jnp.bfloat16)
    grad_t = grad.T
    row_dot = jnp.sum(grad_t.astype(jnp.float32) * out_t.astype(jnp.float32), axis=0, keepdims=True)
    for g in range(GROUP):
        here = row_dot[:, lanes[g]]
        for rows in blocks:
            slope_ref[rows, lanes[g]] = (
                score_ref[rows, lanes[g]] * (cross_ref[rows, lanes[g]] - here)
            ).astype(jnp.bfloat16)
    sink_grad_ref[pl.ds(kv_head, 1), :] = jnp.concatenate(sink_weights, axis=1) * row_dot
    out = out_t.T
    grad_query = (dot(keys.T, slope_ref[...], NN) * FACTOR).astype(jnp.bfloat16).T
    for g in range(GROUP):
        cols = slice(g * HEAD_DIM, (g + 1) * HEAD_DIM)
        out_ref[:, cols] = out[lanes[g], :]
        grad_query_ref[:, cols] = grad_query[lanes[g], :]
    grad_key = dot(slope_ref[...], query, NN) * FACTOR
    grad_value = dot(weight_ref[...], grad, NN)
    for slot, (ref, half) in enumerate(
        [
            (near_ref, 0),
            (near_ref, 1),
            (far2_ref, 0),
            (far2_ref, 1),
            (far4_ref, 0),
            (far4_ref, 1),
            (far6_ref, 0),
            (far6_ref, 1),
        ]
    ):
        start = half * 2 * TOK
        ref[start : start + TOK, :] = grad_key[blocks[slot], :].astype(ref.dtype)
        ref[start + TOK : start + 2 * TOK, :] = grad_value[blocks[slot], :].astype(ref.dtype)


def attention(marks, sink_logits, bias, queries, cotangent, packs):
    wide = pl.BlockSpec((TOK, GROUP_COLS), lambda h: (0, h))
    pack_spec = pl.BlockSpec((PACK_ROWS, HEAD_DIM), lambda h: (0, h))
    pair_spec = pl.BlockSpec((4 * TOK, HEAD_DIM), lambda h: (0, h))
    smem = pl.BlockSpec(memory_space=pltpu.SMEM)
    pair_shape = (4 * TOK, KV_COLS)
    return pl.pallas_call(
        attention_kernel,
        grid=(KV_HEADS,),
        in_specs=[smem, smem, pl.BlockSpec((TOK, TOK), lambda h: (0, 0)), wide, wide]
        + [pack_spec] * MOST,
        out_specs=[
            wide,
            wide,
            pair_spec,
            pair_spec,
            pair_spec,
            pair_spec,
            pl.BlockSpec((KV_HEADS, GROUP_COLS), lambda h: (0, 0)),
        ],
        out_shape=[
            jax.ShapeDtypeStruct((TOK, HEADS * HEAD_DIM), jnp.bfloat16),
            jax.ShapeDtypeStruct((TOK, HEADS * HEAD_DIM), jnp.bfloat16),
            jax.ShapeDtypeStruct(pair_shape, jnp.float32),
            jax.ShapeDtypeStruct(pair_shape, jnp.bfloat16),
            jax.ShapeDtypeStruct(pair_shape, jnp.bfloat16),
            jax.ShapeDtypeStruct(pair_shape, jnp.bfloat16),
            jax.ShapeDtypeStruct((KV_HEADS, GROUP_COLS), jnp.float32),
        ],
        scratch_shapes=[
            pltpu.VMEM((WIN, TOK), jnp.float32),
            pltpu.VMEM((WIN, GROUP_COLS), jnp.float32),
            pltpu.VMEM((WIN, GROUP_COLS), jnp.float32),
            pltpu.VMEM((WIN, GROUP_COLS), jnp.bfloat16),
            pltpu.VMEM((WIN, GROUP_COLS), jnp.bfloat16),
        ],
        compiler_params=pltpu.CompilerParams(
            dimension_semantics=("arbitrary",), vmem_limit_bytes=20 << 20
        ),
        cost_estimate=pl.CostEstimate(
            flops=10 * HEADS * TOK * WIN * HEAD_DIM,
            transcendentals=HEADS * TOK * WIN,
            bytes_accessed=8 << 20,
        ),
        name="attention",
    )(marks, sink_logits, bias, queries, cotangent, *packs)


def body(queries, key_rows, value_rows, cotangent, sink_logits, run_lengths, segment_ids):
    n_ctx = lax.axis_size(CTX)
    ctx_index = lax.axis_index(CTX)
    segments = segment_ids[0]
    mark_rows = jnp.broadcast_to(
        segments.astype(jnp.bfloat16)[None, None, :], (8, KV_HEADS, TOK)
    ).reshape(8, KV_COLS)
    own = jnp.concatenate([key_rows[0], value_rows[0], mark_rows], axis=0)
    own = lax.optimization_barrier(own)

    packs = [own] + [None] * (MOST - 1)
    packs[1] = passed_along(own, 1)
    for by in (6, 4, 2):
        packs[by] = passed_along(own, by)
    for by in (6, 4, 2):
        packs[by + 1] = passed_along(packs[1], by)

    run_ends = jnp.cumsum(run_lengths[0])
    before = run_ends <= ctx_index
    run_start = jnp.max(jnp.where(before, run_ends, 0))
    first_mark = segments[0]
    first_count = jnp.sum((segments == first_mark).astype(jnp.int32))
    marks = jnp.stack([ctx_index - run_start, first_mark, first_count]).astype(jnp.int32)
    positions = jnp.arange(TOK, dtype=jnp.int32)
    seen = (segments[:, None] == segments[None, :]) & (
        positions[:, None] <= positions[None, :]
    )
    bias = jnp.where(seen, 0.0, -jnp.inf).astype(jnp.float32)

    attended, grad_query, near, far2, far4, far6, sink_rows = attention(
        marks, sink_logits, bias, queries[0], cotangent[0], packs
    )
    returned = []
    for by, far in ((6, far6), (4, far4), (2, far2)):
        returned.append(passed_along(far, -by))
    grad_sink = -jnp.sum(sink_rows.reshape(HEADS, TOK), axis=1)
    grad_sink = lax.psum(grad_sink, ("ctx_2", "dp_0"))
    near = near + sum(part.astype(jnp.float32) for part in returned)
    last = passed_along(near[2 * TOK :].astype(jnp.bfloat16), -1)
    grad_sink, _ = lax.optimization_barrier((grad_sink, near))
    grad_sink = lax.psum(grad_sink, "ctx_0")
    grad_sink = lax.psum(grad_sink, "ctx_1")
    grad_sink = lax.psum(grad_sink, "dp_1")
    grad_kv = (near[: 2 * TOK] + last.astype(jnp.float32)).astype(jnp.bfloat16)
    scale_down = 1.0 / math.sqrt(lax.axis_size(DP) * n_ctx * TOK)
    return (
        attended[None],
        grad_query[None],
        grad_kv[:TOK][None],
        grad_kv[TOK:][None],
        grad_sink * scale_down,
    )


def solution(mesh):
    split = Mesh(mesh.devices.reshape(8, 2, 8, 4, 2), ("dp_0", "dp_1", "ctx_0", "ctx_1", "ctx_2"))
    in_specs = (
        P(DP, CTX, None),
        P(DP, CTX, None),
        P(DP, CTX, None),
        P(DP, CTX, None),
        P(),
        P(DP, None),
        P(DP, CTX),
    )
    out_specs = (P(DP, CTX, None), P(DP, CTX, None), P(DP, CTX, None), P(DP, CTX, None), P())
    return jax.shard_map(body, mesh=split, in_specs=in_specs, out_specs=out_specs, check_vma=False)
```

profile of v0, /device:TPU:1, one launch (start us, length us, event | category | flops | bytes accessed | tf_op | source)
XLA Modules:
  0.0 207.3 jit_solution(5609090508468317933)
XLA Ops:
  0.6 0.7 bitcast_convert_fusion
  1.4 1.0 pad_maximum_fusion.refs_0_
  2.4 19.9 %collective-permute-start = (bf16[264,512]{1,0:T(8,128)(2,1)S(1)}, bf16[264,512]{1,0:T(8,128)(2,1)S(1)}, u32[]{:S(2)}, u32[]{:S(2)}) collective-permute-start(bf16[264,512]{1,0:T(8,128)(2,1)S(1)} %pad_maximum_fusion.refs_0_), channel_id=1, source_target_pairs={{0,1},{1,2},{2,3},{3,4},{4,5},{5,6},{6,7},{7,8},{8,9},{9,10},{10,1... | collective-permute-start | bytes 811016 | tf_op jit(solution)/shard_map/ppermute | solution.py:34
  22.3 4.4 %collective-permute-start.5 = (bf16[264,512]{1,0:T(8,128)(2,1)S(1)}, bf16[264,512]{1,0:T(8,128)(2,1)S(1)}, u32[]{:S(2)}, u32[]{:S(2)}) collective-permute-start(bf16[264,512]{1,0:T(8,128)(2,1)S(1)} %pad_maximum_fusion.refs_0_), channel_id=1, source_target_pairs={{0,6},{1,7},{2,8},{3,9},{4,10},{5,11},{6,12},{7,13},{8,14},{9,15},... | collective-permute-start | bytes 811016 | tf_op jit(solution)/shard_map/ppermute | solution.py:34
  26.7 3.5 %collective-permute-start.3 = (bf16[264,512]{1,0:T(8,128)(2,1)S(1)}, bf16[264,512]{1,0:T(8,128)(2,1)S(1)}, u32[]{:S(2)}, u32[]{:S(2)}) collective-permute-start(bf16[264,512]{1,0:T(8,128)(2,1)S(1)} %pad_maximum_fusion.refs_0_), channel_id=1, source_target_pairs={{0,4},{1,5},{2,6},{3,7},{4,8},{5,9},{6,10},{7,11},{8,12},{9,13},{1... | collective-permute-start | bytes 811016 | tf_op jit(solution)/shard_map/ppermute | solution.py:34
  30.1 2.5 %collective-permute-start.1 = (bf16[264,512]{1,0:T(8,128)(2,1)S(1)}, bf16[264,512]{1,0:T(8,128)(2,1)S(1)}, u32[]{:S(2)}, u32[]{:S(2)}) collective-permute-start(bf16[264,512]{1,0:T(8,128)(2,1)S(1)} %pad_maximum_fusion.refs_0_), channel_id=1, source_target_pairs={{0,2},{1,3},{2,4},{3,5},{4,6},{5,7},{6,8},{7,9},{8,10},{9,11},{10,... | collective-permute-start | bytes 811016 | tf_op jit(solution)/shard_map/ppermute | solution.py:34
  36.2 5.0 %collective-permute-start.6 = (bf16[264,512]{1,0:T(8,128)(2,1)S(1)}, bf16[264,512]{1,0:T(8,128)(2,1)S(1)}, u32[]{:S(2)}, u32[]{:S(2)}) collective-permute-start(bf16[264,512]{1,0:T(8,128)(2,1)S(1)} %collective-permute-done.refs_1_), channel_id=1, source_target_pairs={{0,6},{1,7},{2,8},{3,9},{4,10},{5,11},{6,12},{7,13},{8,14},{9,15},... | collective-permute-start | bytes 811016 | tf_op jit(solution)/shard_map/ppermute | solution.py:34
  41.2 3.2 %collective-permute-start.4 = (bf16[264,512]{1,0:T(8,128)(2,1)S(1)}, bf16[264,512]{1,0:T(8,128)(2,1)S(1)}, u32[]{:S(2)}, u32[]{:S(2)}) collective-permute-start(bf16[264,512]{1,0:T(8,128)(2,1)S(1)} %collective-permute-done.refs_1_), channel_id=1, source_target_pairs={{0,4},{1,5},{2,6},{3,7},{4,8},{5,9},{6,10},{7,11},{8,12},{9,13},{1... | collective-permute-start | bytes 811016 | tf_op jit(solution)/shard_map/ppermute | solution.py:34
  44.3 1.9 collective-permute-start.2
  46.3 0.7 pad_add_fusion.marks_ref
  47.1 3.7 %collective-permute-done.6.refs_7_ = bf16[264,512]{1,0:T(8,128)(2,1)S(1)} collective-permute-done((bf16[264,512]{1,0:T(8,128)(2,1)S(1)}, bf16[264,512]{1,0:T(8,128)(2,1)S(1)}, u32[]{:S(2)}, u32[]{:S(2)}) %collective-permute-start.6) | collective-permute-done | bytes 270368 | tf_op jit(solution)/shard_map/ppermute | solution.py:34
  50.8 3.0 %collective-permute-done.2.refs_3_ = bf16[264,512]{1,0:T(8,128)(2,1)S(1)} collective-permute-done((bf16[264,512]{1,0:T(8,128)(2,1)S(1)}, bf16[264,512]{1,0:T(8,128)(2,1)S(1)}, u32[]{:S(2)}, u32[]{:S(2)}) %collective-permute-start.2) | collective-permute-done | bytes 270368 | tf_op jit(solution)/shard_map/ppermute | solution.py:34
  54.5 1.0 copy-done.1
  55.5 13.5 %attention.1 = (bf16[128,2048]{1,0:T(8,128)(2,1)}, bf16[128,2048]{1,0:T(8,128)(2,1)}, f32[512,512]{1,0:T(8,128)S(1)}, bf16[512,512]{1,0:T(8,128)(2,1)S(1)}, bf16...) custom-call(s32[3]{0:T(128)S(1)} %pad_add_fusion.marks_ref, f32[16]{0:T(128)S(1)} %copy-done.2, ...), custom_call_target="tpu_custom_call" | custom-call | flops 2684354560 | bytes 8388608 | tf_op jit(solution)/shard_map/attention/pallas_call | solution.py:146
  69.0 1.3 collective-permute-start.7
  70.3 1.3 collective-permute-start.8
  71.6 1.3 collective-permute-start.9
  72.9 24.4 %collective-permute-done.7 = bf16[512,512]{1,0:T(8,128)(2,1)S(1)} collective-permute-done((bf16[512,512]{1,0:T(8,128)(2,1)S(1)}, bf16[512,512]{1,0:T(8,128)(2,1)S(1)}, u32[]{:S(2)}, u32[]{:S(2)}) %collective-permute-start.7) | collective-permute-done | bytes 524320 | tf_op jit(solution)/shard_map/ppermute | solution.py:34
  97.3 1.6 collective-permute-done.8
  99.2 1.3 collective-permute-start.10
  100.7 49.8 %psum.28 = f32[16]{0:T(128)S(1)} all-reduce(f32[16]{0:T(128)S(1)} %neg.3), channel_id=1, replica_groups=mesh['dp_0'=8,'dp_1'=2,'ctx_0'=8,'ctx_1'=4,'ctx_2'=2] {'ctx_2','dp_0'}, use_global_device_ids=true, to_apply=%region_4.5 | all-reduce | flops 16 | bytes 128 | tf_op jit(solution)/shard_map/psum | solution.py:224
  150.4 32.1 %psum.29 = f32[16]{0:T(128)S(1)} all-reduce(f32[16]{0:T(128)S(1)} %psum.28), channel_id=1, replica_groups=mesh['dp_0'=8,'dp_1'=2,'ctx_0'=8,'ctx_1'=4,'ctx_2'=2] {'ctx_0'}, use_global_device_ids=true, to_apply=%region_5.6 | all-reduce | flops 16 | bytes 128 | tf_op jit(solution)/shard_map/psum | solution.py:228
  182.5 9.3 %psum.30 = f32[16]{0:T(128)S(1)} all-reduce(f32[16]{0:T(128)S(1)} %psum.29), channel_id=1, replica_groups=mesh['dp_0'=8,'dp_1'=2,'ctx_0'=8,'ctx_1'=4,'ctx_2'=2] {'ctx_1'}, use_global_device_ids=true, to_apply=%region_6.7 | all-reduce | flops 16 | bytes 128 | tf_op jit(solution)/shard_map/psum | solution.py:229
  191.8 14.2 %psum.31 = f32[16]{0:T(128)S(1)} all-reduce(f32[16]{0:T(128)S(1)} %psum.30), channel_id=1, replica_groups=mesh['dp_0'=8,'dp_1'=2,'ctx_0'=8,'ctx_1'=4,'ctx_2'=2] {'dp_1'}, use_global_device_ids=true, to_apply=%region_7.8 | all-reduce | flops 16 | bytes 128 | tf_op jit(solution)/shard_map/psum | solution.py:230
  (32 shorter events, 5.3 us)
Async XLA Ops:
  0.6 53.2 %copy-start = (bf16[1,128,2048]{2,1,0:T(8,128)(2,1)S(1)}, bf16[1,128,2048]{2,1,0:T(8,128)(2,1)}, u32[]{:S(2)}) copy-start(bf16[1,128,2048]{2,1,0:T(8,128)(2,1)} %param.7) | copy-start | bytes 1572868
  2.4 33.8 %collective-permute-start = (bf16[264,512]{1,0:T(8,128)(2,1)S(1)}, bf16[264,512]{1,0:T(8,128)(2,1)S(1)}, u32[]{:S(2)}, u32[]{:S(2)}) collective-permute-start(bf16[264,512]{1,0:T(8,128)(2,1)S(1)} %pad_maximum_fusion.refs_0_), channel_id=1, source_target_pairs={{0,1},{1,2},{2,3},{3,4},{4,5},{5,6},{6,7},{7,8},{8,9},{9,10},{10,1... | collective-permute-start | bytes 811016 | tf_op jit(solution)/shard_map/ppermute | solution.py:34
  22.3 22.0 %collective-permute-start.5 = (bf16[264,512]{1,0:T(8,128)(2,1)S(1)}, bf16[264,512]{1,0:T(8,128)(2,1)S(1)}, u32[]{:S(2)}, u32[]{:S(2)}) collective-permute-start(bf16[264,512]{1,0:T(8,128)(2,1)S(1)} %pad_maximum_fusion.refs_0_), channel_id=1, source_target_pairs={{0,6},{1,7},{2,8},{3,9},{4,10},{5,11},{6,12},{7,13},{8,14},{9,15},... | collective-permute-start | bytes 811016 | tf_op jit(solution)/shard_map/ppermute | solution.py:34
  26.7 20.4 %collective-permute-start.3 = (bf16[264,512]{1,0:T(8,128)(2,1)S(1)}, bf16[264,512]{1,0:T(8,128)(2,1)S(1)}, u32[]{:S(2)}, u32[]{:S(2)}) collective-permute-start(bf16[264,512]{1,0:T(8,128)(2,1)S(1)} %pad_maximum_fusion.refs_0_), channel_id=1, source_target_pairs={{0,4},{1,5},{2,6},{3,7},{4,8},{5,9},{6,10},{7,11},{8,12},{9,13},{1... | collective-permute-start | bytes 811016 | tf_op jit(solution)/shard_map/ppermute | solution.py:34
  30.1 16.9 %collective-permute-start.1 = (bf16[264,512]{1,0:T(8,128)(2,1)S(1)}, bf16[264,512]{1,0:T(8,128)(2,1)S(1)}, u32[]{:S(2)}, u32[]{:S(2)}) collective-permute-start(bf16[264,512]{1,0:T(8,128)(2,1)S(1)} %pad_maximum_fusion.refs_0_), channel_id=1, source_target_pairs={{0,2},{1,3},{2,4},{3,5},{4,6},{5,7},{6,8},{7,9},{8,10},{9,11},{10,... | collective-permute-start | bytes 811016 | tf_op jit(solution)/shard_map/ppermute | solution.py:34
  32.7 0.7 copy-start.4
  34.9 0.7 copy-start.3
  36.2 14.6 %collective-permute-start.6 = (bf16[264,512]{1,0:T(8,128)(2,1)S(1)}, bf16[264,512]{1,0:T(8,128)(2,1)S(1)}, u32[]{:S(2)}, u32[]{:S(2)}) collective-permute-start(bf16[264,512]{1,0:T(8,128)(2,1)S(1)} %collective-permute-done.refs_1_), channel_id=1, source_target_pairs={{0,6},{1,7},{2,8},{3,9},{4,10},{5,11},{6,12},{7,13},{8,14},{9,15},... | collective-permute-start | bytes 811016 | tf_op jit(solution)/shard_map/ppermute | solution.py:34
  41.2 9.7 %collective-permute-start.4 = (bf16[264,512]{1,0:T(8,128)(2,1)S(1)}, bf16[264,512]{1,0:T(8,128)(2,1)S(1)}, u32[]{:S(2)}, u32[]{:S(2)}) collective-permute-start(bf16[264,512]{1,0:T(8,128)(2,1)S(1)} %collective-permute-done.refs_1_), channel_id=1, source_target_pairs={{0,4},{1,5},{2,6},{3,7},{4,8},{5,9},{6,10},{7,11},{8,12},{9,13},{1... | collective-permute-start | bytes 811016 | tf_op jit(solution)/shard_map/ppermute | solution.py:34
  44.3 9.5 %collective-permute-start.2 = (bf16[264,512]{1,0:T(8,128)(2,1)S(1)}, bf16[264,512]{1,0:T(8,128)(2,1)S(1)}, u32[]{:S(2)}, u32[]{:S(2)}) collective-permute-start(bf16[264,512]{1,0:T(8,128)(2,1)S(1)} %collective-permute-done.refs_1_), channel_id=1, source_target_pairs={{0,2},{1,3},{2,4},{3,5},{4,6},{5,7},{6,8},{7,9},{8,10},{9,11},{10,... | collective-permute-start | bytes 811016 | tf_op jit(solution)/shard_map/ppermute | solution.py:34
  53.8 0.7 copy-start.2
  54.5 1.0 copy-start.1
  69.0 28.3 %collective-permute-start.7 = (bf16[512,512]{1,0:T(8,128)(2,1)S(1)}, bf16[512,512]{1,0:T(8,128)(2,1)S(1)}, u32[]{:S(2)}, u32[]{:S(2)}) collective-permute-start(bf16[512,512]{1,0:T(8,128)(2,1)S(1)} %get-tuple-element.16), channel_id=1, source_target_pairs={{6,0},{7,1},{8,2},{9,3},{10,4},{11,5},{12,6},{13,7},{14,8},{15,9},... | collective-permute-start | bytes 1572872 | tf_op jit(solution)/shard_map/ppermute | solution.py:34
  70.3 28.6 %collective-permute-start.8 = (bf16[512,512]{1,0:T(8,128)(2,1)S(1)}, bf16[512,512]{1,0:T(8,128)(2,1)S(1)}, u32[]{:S(2)}, u32[]{:S(2)}) collective-permute-start(bf16[512,512]{1,0:T(8,128)(2,1)S(1)} %get-tuple-element.17), channel_id=1, source_target_pairs={{4,0},{5,1},{6,2},{7,3},{8,4},{9,5},{10,6},{11,7},{12,8},{13,9},{1... | collective-permute-start | bytes 1572872 | tf_op jit(solution)/shard_map/ppermute | solution.py:34
  71.6 27.3 %collective-permute-start.9 = (bf16[512,512]{1,0:T(8,128)(2,1)S(1)}, bf16[512,512]{1,0:T(8,128)(2,1)S(1)}, u32[]{:S(2)}, u32[]{:S(2)}) collective-permute-start(bf16[512,512]{1,0:T(8,128)(2,1)S(1)} %get-tuple-element.18), channel_id=1, source_target_pairs={{2,0},{3,1},{4,2},{5,3},{6,4},{7,5},{8,6},{9,7},{10,8},{11,9},{12,... | collective-permute-start | bytes 1572872 | tf_op jit(solution)/shard_map/ppermute | solution.py:34
  99.2 107.3 %collective-permute-start.10 = (bf16[256,512]{1,0:T(8,128)(2,1)S(1)}, bf16[256,512]{1,0:T(8,128)(2,1)S(1)}, u32[]{:S(2)}, u32[]{:S(2)}) collective-permute-start(bf16[256,512]{1,0:T(8,128)(2,1)S(1)} %slice.35), channel_id=1, source_target_pairs={{1,0},{2,1},{3,2},{4,3},{5,4},{6,5},{7,6},{8,7},{9,8},{10,9},{11,1... | collective-permute-start | bytes 786440 | tf_op jit(solution)/shard_map/ppermute | solution.py:34
where the time goes:
time: 208 us; the launch traced here: 207 us
  blocking collectives  105 us (50%)
  starting transfers between devices  45.5 us (22%)
  waiting for transfers between devices  32.8 us (16%)
  Pallas kernels  13.5 us (6%)
  other arithmetic  4.93 us (2%)
  local copies, waits for them, and re-layouts  3.85 us (2%)
    psum x1, blocking collectives, body(): grad_sink = lax.psum(grad_sink, ('ctx_2', 'dp_0'))  49.8 us
    ppermute x11, starting transfers between devices, passed_along(): return lax.ppermute(array, CTX, pairs)  45.5 us
    ppermute x11, waiting for transfers between devices, passed_along(): return lax.ppermute(array, CTX, pairs)  32.8 us
    psum x1, blocking collectives, body(): grad_sink = lax.psum(grad_sink, 'ctx_0')  32.1 us
    psum x1, blocking collectives, body(): grad_sink = lax.psum(grad_sink, 'dp_1')  14.2 us
    pallas_call x1, Pallas kernels, attention(): pl.pallas_call(attention_kernel, grid=(KV_HEADS,), in_specs=[smem, smem,...  13.5 us
    psum x1, blocking collectives, body(): grad_sink = lax.psum(grad_sink, 'ctx_1')  9.25 us
  transfers between devices with their start and end apart: 11, of which 4 were waited for; matrix products, arithmetic and copies ran while one was open for 1% of the time, Pallas kernels for 0%

commit v1 on v0

--- a/solution.py
+++ b/solution.py
@@ -1,3 +1,4 @@
+import functools
 import math
 
 import jax
@@ -19,6 +20,11 @@
 PACK_ROWS = 2 * TOK + 8
 WIN = MOST * TOK
 GROUP_COLS = GROUP * HEAD_DIM
+Z_MEMBERS = 16
+PLANE_MEMBERS = 64
+CHUNKS = 2
+CHUNK_HEADS = KV_HEADS // CHUNKS
+CHUNK_COLS = CHUNK_HEADS * HEAD_DIM
 FACTOR = HEAD_DIM ** (-0.5)
 CTX = ("ctx_0", "ctx_1", "ctx_2")
 DP = ("dp_0", "dp_1")
@@ -39,33 +45,49 @@
 
 
 def attention_kernel(
+    fresh,
+    first_head,
+    place_ref,
+    runs_ref,
+    sink_ref,
     marks_ref,
-    sink_ref,
-    bias_ref,
     query_ref,
     grad_ref,
     *refs,
 ):
     packs = refs[:MOST]
-    (out_ref, grad_query_ref, near_ref, far2_ref, far4_ref, far6_ref, sink_grad_ref) = refs[
-        MOST : MOST + 7
-    ]
-    mask_ref, score_ref, cross_ref, weight_ref, slope_ref = refs[MOST + 7 :]
-    kv_head = pl.program_id(0)
-
-    @pl.when(kv_head == 0)
+    sink_in_ref = None if fresh else refs[MOST + 2]
+    refs = refs[MOST:] if fresh else refs[MOST + 3 :]
+    (out_ref, grad_query_ref, near_ref, far2_ref, far4_ref, far6_ref, sink_grad_ref) = refs[:7]
+    mask_ref, score_ref, cross_ref, weight_ref, slope_ref = refs[7:]
+    step = pl.program_id(0)
+
+    @pl.when(step == 0)
     def _():
-        mask_ref[:TOK, :] = bias_ref[...]
+        if fresh:
+            sink_grad_ref[...] = jnp.zeros_like(sink_grad_ref)
+        else:
+            sink_grad_ref[...] = sink_in_ref[...]
+        place = place_ref[0]
+        ends = jnp.int32(0)
+        run_start = jnp.int32(0)
+        for run in range(runs_ref.shape[0]):
+            ends = ends + runs_ref[run]
+            run_start = jnp.where(ends <= place, ends, run_start)
+        reach = place - run_start
         rows = lax.broadcasted_iota(jnp.int32, (TOK, TOK), 0)
         cols = lax.broadcasted_iota(jnp.int32, (TOK, TOK), 1)
-        reach = marks_ref[0]
-        first_mark = marks_ref[1].astype(jnp.float32)
-        first_count = marks_ref[2]
+        marks = marks_ref[...].astype(jnp.float32)
+        wide = jnp.broadcast_to(marks, (TOK, TOK))
+        seen = (wide.T == wide) & (rows <= cols)
+        mask_ref[:TOK, :] = jnp.where(seen, 0.0, -jnp.inf)
+        first_mark = marks[:, :1]
+        first_part = wide == jnp.broadcast_to(first_mark, (TOK, TOK))
         for slot in range(1, MOST):
             row = packs[slot][2 * TOK : 2 * TOK + 8, :].astype(jnp.float32)[:1, :]
             same = jnp.sum((row == first_mark).astype(jnp.float32), axis=1, keepdims=True)
             same = jnp.where(slot <= reach, same, 0.0)
-            seen = (rows >= TOK - same.astype(jnp.int32)) & (cols < first_count)
+            seen = (rows >= TOK - same.astype(jnp.int32)) & first_part
             mask_ref[slot * TOK : (slot + 1) * TOK, :] = jnp.where(seen, 0.0, -jnp.inf)
 
     def stacked(ref):
@@ -83,7 +105,7 @@
     lanes = [slice(g * TOK, (g + 1) * TOK) for g in range(GROUP)]
     sink_weights = []
     for g in range(GROUP):
-        sink = sink_ref[kv_head * GROUP + g]
+        sink = sink_ref[step * GROUP + g]
         best = jnp.full((8, TOK), sink, jnp.float32)
         for rows in blocks:
             scores = score_ref[rows, lanes[g]] * FACTOR + mask_ref[rows, :]
@@ -111,7 +133,12 @@
             slope_ref[rows, lanes[g]] = (
                 score_ref[rows, lanes[g]] * (cross_ref[rows, lanes[g]] - here)
             ).astype(jnp.bfloat16)
-    sink_grad_ref[pl.ds(kv_head, 1), :] = jnp.concatenate(sink_weights, axis=1) * row_dot
+    head_lane = lax.broadcasted_iota(jnp.int32, (1, TOK), 1) - (first_head + step * GROUP)
+    sink_row = jnp.zeros((1, TOK), jnp.float32)
+    for g in range(GROUP):
+        part = jnp.sum(sink_weights[g] * row_dot[:, lanes[g]], axis=1, keepdims=True)
+        sink_row = sink_row - jnp.where(head_lane == g, part, 0.0)
+    sink_grad_ref[...] = sink_grad_ref[...] + sink_row
     out = out_t.T
     grad_query = (dot(keys.T, slope_ref[...], NN) * FACTOR).astype(jnp.bfloat16).T
     for g in range(GROUP):
@@ -137,17 +164,23 @@
         ref[start + TOK : start + 2 * TOK, :] = grad_value[blocks[slot], :].astype(ref.dtype)
 
 
-def attention(marks, sink_logits, bias, queries, cotangent, packs):
-    wide = pl.BlockSpec((TOK, GROUP_COLS), lambda h: (0, h))
-    pack_spec = pl.BlockSpec((PACK_ROWS, HEAD_DIM), lambda h: (0, h))
+def attention(chunk, place, runs, sink_logits, marks, queries, cotangent, packs, written):
+    first = chunk * CHUNK_HEADS
+    wide = pl.BlockSpec((TOK, GROUP_COLS), lambda h: (0, first + h))
+    whole_pack = pl.BlockSpec((PACK_ROWS, HEAD_DIM), lambda h: (0, first + h))
+    chunk_pack = pl.BlockSpec((PACK_ROWS, HEAD_DIM), lambda h: (0, h))
     pair_spec = pl.BlockSpec((4 * TOK, HEAD_DIM), lambda h: (0, h))
     smem = pl.BlockSpec(memory_space=pltpu.SMEM)
-    pair_shape = (4 * TOK, KV_COLS)
+    pair_shape = (4 * TOK, CHUNK_COLS)
+    heads = CHUNK_HEADS * GROUP
+    sink_spec = pl.BlockSpec((Z_MEMBERS, TOK), lambda h: (0, 0))
+    n_fixed = 6 + MOST
     return pl.pallas_call(
-        attention_kernel,
-        grid=(KV_HEADS,),
-        in_specs=[smem, smem, pl.BlockSpec((TOK, TOK), lambda h: (0, 0)), wide, wide]
-        + [pack_spec] * MOST,
+        functools.partial(attention_kernel, not written, first * GROUP),
+        grid=(CHUNK_HEADS,),
+        in_specs=[smem, smem, smem, pl.BlockSpec((1, TOK), lambda h: (0, 0)), wide, wide]
+        + [chunk_pack if pack.shape[1] == CHUNK_COLS else whole_pack for pack in packs]
+        + ([pl.BlockSpec(memory_space=pl.ANY)] * 2 + [sink_spec] if written else []),
         out_specs=[
             wide,
             wide,
@@ -155,7 +188,7 @@
             pair_spec,
             pair_spec,
             pair_spec,
-            pl.BlockSpec((KV_HEADS, GROUP_COLS), lambda h: (0, 0)),
+            sink_spec,
         ],
         out_shape=[
             jax.ShapeDtypeStruct((TOK, HEADS * HEAD_DIM), jnp.bfloat16),
@@ -164,7 +197,7 @@
             jax.ShapeDtypeStruct(pair_shape, jnp.bfloat16),
             jax.ShapeDtypeStruct(pair_shape, jnp.bfloat16),
             jax.ShapeDtypeStruct(pair_shape, jnp.bfloat16),
-            jax.ShapeDtypeStruct((KV_HEADS, GROUP_COLS), jnp.float32),
+            jax.ShapeDtypeStruct((Z_MEMBERS, TOK), jnp.float32),
         ],
         scratch_shapes=[
             pltpu.VMEM((WIN, TOK), jnp.float32),
@@ -173,62 +206,86 @@
             pltpu.VMEM((WIN, GROUP_COLS), jnp.bfloat16),
             pltpu.VMEM((WIN, GROUP_COLS), jnp.bfloat16),
         ],
+        input_output_aliases={n_fixed: 0, n_fixed + 1: 1} if written else {},
         compiler_params=pltpu.CompilerParams(
             dimension_semantics=("arbitrary",), vmem_limit_bytes=20 << 20
         ),
         cost_estimate=pl.CostEstimate(
-            flops=10 * HEADS * TOK * WIN * HEAD_DIM,
-            transcendentals=HEADS * TOK * WIN,
-            bytes_accessed=8 << 20,
+            flops=10 * heads * TOK * WIN * HEAD_DIM,
+            transcendentals=heads * TOK * WIN,
+            bytes_accessed=4 << 20,
         ),
-        name="attention",
-    )(marks, sink_logits, bias, queries, cotangent, *packs)
+    )(
+        place,
+        runs,
+        lax.slice(sink_logits, (first * GROUP,), (first * GROUP + heads,)),
+        marks,
+        queries,
+        cotangent,
+        *packs,
+        *written,
+    )
+
+
+def exchanged(spread, axes):
+    return jnp.sum(lax.all_to_all(spread, axes, 0, 0, tiled=True), axis=0)
 
 
 def body(queries, key_rows, value_rows, cotangent, sink_logits, run_lengths, segment_ids):
     n_ctx = lax.axis_size(CTX)
-    ctx_index = lax.axis_index(CTX)
-    segments = segment_ids[0]
+    place = lax.axis_index(CTX).astype(jnp.int32).reshape(1)
+    place, segment_ids = lax.optimization_barrier((place, segment_ids))
     mark_rows = jnp.broadcast_to(
-        segments.astype(jnp.bfloat16)[None, None, :], (8, KV_HEADS, TOK)
+        segment_ids[0].astype(jnp.bfloat16)[None, None, :], (8, KV_HEADS, TOK)
     ).reshape(8, KV_COLS)
-    own = jnp.concatenate([key_rows[0], value_rows[0], mark_rows], axis=0)
-    own = lax.optimization_barrier(own)
-
-    packs = [own] + [None] * (MOST - 1)
-    packs[1] = passed_along(own, 1)
+
+    def packed(start, stop):
+        parts = (key_rows[0], value_rows[0], mark_rows)
+        return jnp.concatenate([part[:, start:stop] for part in parts], axis=0)
+
+    near_odd = []
+    for chunk in range(CHUNKS):
+        mine = packed(chunk * CHUNK_COLS, (chunk + 1) * CHUNK_COLS)
+        near_odd.append(passed_along(mine, 1))
+    own = packed(0, KV_COLS)
+    evens = {0: own}
     for by in (6, 4, 2):
-        packs[by] = passed_along(own, by)
-    for by in (6, 4, 2):
-        packs[by + 1] = passed_along(packs[1], by)
-
-    run_ends = jnp.cumsum(run_lengths[0])
-    before = run_ends <= ctx_index
-    run_start = jnp.max(jnp.where(before, run_ends, 0))
-    first_mark = segments[0]
-    first_count = jnp.sum((segments == first_mark).astype(jnp.int32))
-    marks = jnp.stack([ctx_index - run_start, first_mark, first_count]).astype(jnp.int32)
-    positions = jnp.arange(TOK, dtype=jnp.int32)
-    seen = (segments[:, None] == segments[None, :]) & (
-        positions[:, None] <= positions[None, :]
-    )
-    bias = jnp.where(seen, 0.0, -jnp.inf).astype(jnp.float32)
-
-    attended, grad_query, near, far2, far4, far6, sink_rows = attention(
-        marks, sink_logits, bias, queries[0], cotangent[0], packs
-    )
+        evens[by] = passed_along(own, by)
+    outs = ()
+    sinks = ()
+    kept = []
     returned = []
-    for by, far in ((6, far6), (4, far4), (2, far2)):
-        returned.append(passed_along(far, -by))
-    grad_sink = -jnp.sum(sink_rows.reshape(HEADS, TOK), axis=1)
-    grad_sink = lax.psum(grad_sink, ("ctx_2", "dp_0"))
-    near = near + sum(part.astype(jnp.float32) for part in returned)
-    last = passed_along(near[2 * TOK :].astype(jnp.bfloat16), -1)
-    grad_sink, _ = lax.optimization_barrier((grad_sink, near))
-    grad_sink = lax.psum(grad_sink, "ctx_0")
-    grad_sink = lax.psum(grad_sink, "ctx_1")
-    grad_sink = lax.psum(grad_sink, "dp_1")
-    grad_kv = (near[: 2 * TOK] + last.astype(jnp.float32)).astype(jnp.bfloat16)
+    for chunk in range(CHUNKS):
+        odds = {1: near_odd[chunk]}
+        for by in (6, 4, 2):
+            odds[by + 1] = passed_along(near_odd[chunk], by)
+        packs = [(odds if slot % 2 else evens)[slot] for slot in range(MOST)]
+        *outs, near, far2, far4, far6, sinks = attention(
+            chunk,
+            place,
+            run_lengths[0],
+            sink_logits,
+            segment_ids,
+            queries[0],
+            cotangent[0],
+            packs,
+            (*outs, sinks) if outs else (),
+        )
+        kept.append(near)
+        back = []
+        for by, far in ((6, far6), (4, far4), (2, far2)):
+            back.append(passed_along(far, -by))
+        returned.append(back)
+    attended, grad_query = outs
+    grad_sink = exchanged(sinks, ("ctx_2", "dp_0"))
+    grad_kv = []
+    for chunk in range(CHUNKS):
+        near = kept[chunk] + sum(part.astype(jnp.float32) for part in returned[chunk])
+        last = passed_along(near[2 * TOK :].astype(jnp.bfloat16), -1)
+        grad_kv.append((near[: 2 * TOK] + last.astype(jnp.float32)).astype(jnp.bfloat16))
+    spread = jnp.broadcast_to(grad_sink[None], (PLANE_MEMBERS, TOK))
+    grad_sink = exchanged(spread, ("ctx_0", "ctx_1", "dp_1"))[:HEADS]
+    grad_kv = jnp.concatenate(grad_kv, axis=1)
     scale_down = 1.0 / math.sqrt(lax.axis_size(DP) * n_ctx * TOK)
     return (
         attended[None],

time: 208 us -> 188 us (0.904)
  the two profiles are of different devices: /device:TPU:1 before, /device:TPU:95 now
where the time goes in v1:
time: 188 us; the launch traced here: 187 us
  starting transfers between devices  93.8 us (50%)
  waiting for transfers between devices  47.3 us (25%)
  blocking collectives  24.6 us (13%)
  Pallas kernels  14.5 us (8%)
  local copies, waits for them, and re-layouts  3.07 us (2%)
  other arithmetic  2.64 us (1%)
    ppermute x19, starting transfers between devices, passed_along(): return lax.ppermute(array, CTX, pairs)  78.3 us
    ppermute x19, waiting for transfers between devices, passed_along(): return lax.ppermute(array, CTX, pairs)  47.3 us
    all_to_all x1, blocking collectives, exchanged(): return jnp.sum(lax.all_to_all(spread, axes, 0, 0, tiled=True), axis=0)  24.6 us
    all_to_all x1, starting transfers between devices, exchanged(): return jnp.sum(lax.all_to_all(spread, axes, 0, 0, tiled=True), axis=0)  15.5 us
    pallas_call x2, Pallas kernels, attention(): pl.pallas_call(functools.partial(attention_kernel, not written, first * G...  14.5 us
  transfers between devices with their start and end apart: 20, of which 7 were waited for; matrix products, arithmetic and copies ran while one was open for 1% of the time, Pallas kernels for 4%

profile of v1, /device:TPU:95, one launch (start us, length us, event | category | flops | bytes accessed | tf_op | source)
XLA Modules:
  0.0 186.9 jit_solution(5021928285515567062)
XLA Ops:
  2.4 18.3 %collective-permute-start.7 = (bf16[264,256]{1,0:T(8,128)(2,1)S(1)}, bf16[264,256]{1,0:T(8,128)(2,1)S(1)}, u32[]{:S(2)}, u32[]{:S(2)}) collective-permute-start(bf16[264,256]{1,0:T(8,128)(2,1)S(1)} %get-tuple-element.43), channel_id=1, source_target_pairs={{0,1},{1,2},{2,3},{3,4},{4,5},{5,6},{6,7},{7,8},{8,9},{9,10},{10,1... | collective-permute-start | bytes 405512 | tf_op jit(solution)/shard_map/ppermute | solution.py:40
  20.8 4.3 %collective-permute-start.1 = (bf16[264,512]{1,0:T(8,128)(2,1)S(1)}, bf16[264,512]{1,0:T(8,128)(2,1)S(1)}, u32[]{:S(2)}, u32[]{:S(2)}) collective-permute-start(bf16[264,512]{1,0:T(8,128)(2,1)S(1)} %pad_maximum_fusion.refs_0_), channel_id=1, source_target_pairs={{0,2},{1,3},{2,4},{3,5},{4,6},{5,7},{6,8},{7,9},{8,10},{9,11},{10,... | collective-permute-start | bytes 811016 | tf_op jit(solution)/shard_map/ppermute | solution.py:40
  25.1 1.9 %collective-permute-start = (bf16[264,256]{1,0:T(8,128)(2,1)S(1)}, bf16[264,256]{1,0:T(8,128)(2,1)S(1)}, u32[]{:S(2)}, u32[]{:S(2)}) collective-permute-start(bf16[264,256]{1,0:T(8,128)(2,1)S(1)} %get-tuple-element.44), channel_id=1, source_target_pairs={{0,1},{1,2},{2,3},{3,4},{4,5},{5,6},{6,7},{7,8},{8,9},{9,10},{10,1... | collective-permute-start | bytes 405512 | tf_op jit(solution)/shard_map/ppermute | solution.py:40
  27.1 5.3 %collective-permute-done.7.refs_1_ = bf16[264,256]{1,0:T(8,128)(2,1)S(1)} collective-permute-done((bf16[264,256]{1,0:T(8,128)(2,1)S(1)}, bf16[264,256]{1,0:T(8,128)(2,1)S(1)}, u32[]{:S(2)}, u32[]{:S(2)}) %collective-permute-start.7) | collective-permute-done | bytes 135200 | tf_op jit(solution)/shard_map/ppermute | solution.py:40
  32.3 4.4 %collective-permute-start.10 = (bf16[264,256]{1,0:T(8,128)(2,1)S(1)}, bf16[264,256]{1,0:T(8,128)(2,1)S(1)}, u32[]{:S(2)}, u32[]{:S(2)}) collective-permute-start(bf16[264,256]{1,0:T(8,128)(2,1)S(1)} %collective-permute-done.7.refs_1_), channel_id=1, source_target_pairs={{0,6},{1,7},{2,8},{3,9},{4,10},{5,11},{6,12},{7,13},{8,14},{9,15},... | collective-permute-start | bytes 405512 | tf_op jit(solution)/shard_map/ppermute | solution.py:40
  36.7 4.3 %collective-permute-start.8 = (bf16[264,256]{1,0:T(8,128)(2,1)S(1)}, bf16[264,256]{1,0:T(8,128)(2,1)S(1)}, u32[]{:S(2)}, u32[]{:S(2)}) collective-permute-start(bf16[264,256]{1,0:T(8,128)(2,1)S(1)} %collective-permute-done.7.refs_1_), channel_id=1, source_target_pairs={{0,2},{1,3},{2,4},{3,5},{4,6},{5,7},{6,8},{7,9},{8,10},{9,11},{10,... | collective-permute-start | bytes 405512 | tf_op jit(solution)/shard_map/ppermute | solution.py:40
  41.0 3.5 %collective-permute-start.9 = (bf16[264,256]{1,0:T(8,128)(2,1)S(1)}, bf16[264,256]{1,0:T(8,128)(2,1)S(1)}, u32[]{:S(2)}, u32[]{:S(2)}) collective-permute-start(bf16[264,256]{1,0:T(8,128)(2,1)S(1)} %collective-permute-done.7.refs_1_), channel_id=1, source_target_pairs={{0,4},{1,5},{2,6},{3,7},{4,8},{5,9},{6,10},{7,11},{8,12},{9,13},{1... | collective-permute-start | bytes 405512 | tf_op jit(solution)/shard_map/ppermute | solution.py:40
  44.5 3.7 %collective-permute-start.3 = (bf16[264,512]{1,0:T(8,128)(2,1)S(1)}, bf16[264,512]{1,0:T(8,128)(2,1)S(1)}, u32[]{:S(2)}, u32[]{:S(2)}) collective-permute-start(bf16[264,512]{1,0:T(8,128)(2,1)S(1)} %pad_maximum_fusion.refs_0_), channel_id=1, source_target_pairs={{0,4},{1,5},{2,6},{3,7},{4,8},{5,9},{6,10},{7,11},{8,12},{9,13},{1... | collective-permute-start | bytes 811016 | tf_op jit(solution)/shard_map/ppermute | solution.py:40
  50.2 11.0 %collective-permute-start.2 = (bf16[264,256]{1,0:T(8,128)(2,1)S(1)}, bf16[264,256]{1,0:T(8,128)(2,1)S(1)}, u32[]{:S(2)}, u32[]{:S(2)}) collective-permute-start(bf16[264,256]{1,0:T(8,128)(2,1)S(1)} %collective-permute-done.refs_1_), channel_id=1, source_target_pairs={{0,2},{1,3},{2,4},{3,5},{4,6},{5,7},{6,8},{7,9},{8,10},{9,11},{10,... | collective-permute-start | bytes 405512 | tf_op jit(solution)/shard_map/ppermute | solution.py:40
  65.8 7.2 %shard_map.110 = (bf16[128,2048]{1,0:T(8,128)(2,1)}, bf16[128,2048]{1,0:T(8,128)(2,1)}, f32[512,256]{1,0:T(8,128)S(1)}, bf16[512,256]{1,0:T(8,128)(2,1)S(1)}, bf...) custom-call(s32[1]{0:T(128)} %bitcast.place_ref, s32[16]{0:T(128)S(1)} %bitcast.27, ...), custom_call_target="tpu_custom_call" | custom-call | flops 1342177280 | bytes 4194304 | tf_op jit(solution)/shard_map/pallas_call | solution.py:178
  73.0 7.3 %shard_map.111 = (bf16[128,2048]{1,0:T(8,128)(2,1)}, bf16[128,2048]{1,0:T(8,128)(2,1)}, f32[512,256]{1,0:T(8,128)S(1)}, bf16[512,256]{1,0:T(8,128)(2,1)S(1)}, bf...) custom-call(s32[1]{0:T(128)} %bitcast.place_ref, ...), custom_call_target="tpu_custom_call", output_to_operand_aliasing={{0}: (14, {}), {1}: (15, {})} | custom-call | flops 1342177280 | bytes 4194304 | tf_op jit(solution)/shard_map/pallas_call | solution.py:178
  80.3 24.6 %all_to_all.15 = f32[16,1,128]{2,1,0:T(1,128)S(1)} all-to-all(f32[16,1,128]{2,1,0:T(1,128)S(1)} %bitcast.22), channel_id=1, replica_groups=mesh['dp_0'=8,'dp_1'=2,'ctx_0'=8,'ctx_1'=4,'ctx_2'=2] {'ctx_2','dp_0'}, dimensions={0} | all-to-all | bytes 16384 | tf_op jit(solution)/shard_map/all_to_all | solution.py:231
  105.6 15.5 %all-to-all-start.1 = ((f32[64,1,128]{2,1,0:T(1,128)}), f32[64,1,128]{2,1,0:T(1,128)S(1)}, u32[]{:S(2)}, u32[]{:S(2)}) async-start(f32[64,1,128]{2,1,0:T(1,128)} %broadcast_in_dim.38), calls=%async_computation.1 | async-start | bytes 65536 | tf_op jit(solution)/shard_map/all_to_all | solution.py:231
  121.1 2.2 %collective-permute-start.11 = (bf16[512,256]{1,0:T(8,128)(2,1)S(1)}, bf16[512,256]{1,0:T(8,128)(2,1)S(1)}, u32[]{:S(2)}, u32[]{:S(2)}) collective-permute-start(bf16[512,256]{1,0:T(8,128)(2,1)S(1)} %get-tuple-element.29), channel_id=1, source_target_pairs={{6,0},{7,1},{8,2},{9,3},{10,4},{11,5},{12,6},{13,7},{14,8},{15,9},... | collective-permute-start | bytes 786440 | tf_op jit(solution)/shard_map/ppermute | solution.py:40
  123.3 4.0 %collective-permute-start.12 = (bf16[512,256]{1,0:T(8,128)(2,1)S(1)}, bf16[512,256]{1,0:T(8,128)(2,1)}, u32[]{:S(2)}, u32[]{:S(2)}) collective-permute-start(bf16[512,256]{1,0:T(8,128)(2,1)S(1)} %get-tuple-element.30), channel_id=1, source_target_pairs={{4,0},{5,1},{6,2},{7,3},{8,4},{9,5},{10,6},{11,7},{12,8},{13,9},{1... | collective-permute-start | bytes 786440 | tf_op jit(solution)/shard_map/ppermute | solution.py:40
  127.2 1.9 %collective-permute-start.13 = (bf16[512,256]{1,0:T(8,128)(2,1)S(1)}, bf16[512,256]{1,0:T(8,128)(2,1)}, u32[]{:S(2)}, u32[]{:S(2)}) collective-permute-start(bf16[512,256]{1,0:T(8,128)(2,1)S(1)} %get-tuple-element.31), channel_id=1, source_target_pairs={{2,0},{3,1},{4,2},{5,3},{6,4},{7,5},{8,6},{9,7},{10,8},{11,9},{12,... | collective-permute-start | bytes 786440 | tf_op jit(solution)/shard_map/ppermute | solution.py:40
  129.2 4.6 %collective-permute-start.15 = (bf16[512,256]{1,0:T(8,128)(2,1)S(1)}, bf16[512,256]{1,0:T(8,128)(2,1)S(1)}, u32[]{:S(2)}, u32[]{:S(2)}) collective-permute-start(bf16[512,256]{1,0:T(8,128)(2,1)S(1)} %get-tuple-element.33), channel_id=1, source_target_pairs={{6,0},{7,1},{8,2},{9,3},{10,4},{11,5},{12,6},{13,7},{14,8},{15,9},... | collective-permute-start | bytes 786440 | tf_op jit(solution)/shard_map/ppermute | solution.py:40
  133.7 1.9 %collective-permute-start.16 = (bf16[512,256]{1,0:T(8,128)(2,1)S(1)}, bf16[512,256]{1,0:T(8,128)(2,1)S(1)}, u32[]{:S(2)}, u32[]{:S(2)}) collective-permute-start(bf16[512,256]{1,0:T(8,128)(2,1)S(1)} %get-tuple-element.34), channel_id=1, source_target_pairs={{4,0},{5,1},{6,2},{7,3},{8,4},{9,5},{10,6},{11,7},{12,8},{13,9},{1... | collective-permute-start | bytes 786440 | tf_op jit(solution)/shard_map/ppermute | solution.py:40
  136.2 2.7 %collective-permute-start.17 = (bf16[512,256]{1,0:T(8,128)(2,1)S(1)}, bf16[512,256]{1,0:T(8,128)(2,1)S(1)}, u32[]{:S(2)}, u32[]{:S(2)}) collective-permute-start(bf16[512,256]{1,0:T(8,128)(2,1)S(1)} %get-tuple-element.35), channel_id=1, source_target_pairs={{2,0},{3,1},{4,2},{5,3},{6,4},{7,5},{8,6},{9,7},{10,8},{11,9},{12,... | collective-permute-start | bytes 786440 | tf_op jit(solution)/shard_map/ppermute | solution.py:40
  139.5 5.4 %collective-permute-done.13 = bf16[512,256]{1,0:T(8,128)(2,1)} collective-permute-done((bf16[512,256]{1,0:T(8,128)(2,1)S(1)}, bf16[512,256]{1,0:T(8,128)(2,1)}, u32[]{:S(2)}, u32[]{:S(2)}) %collective-permute-start.13) | collective-permute-done | bytes 262176 | tf_op jit(solution)/shard_map/ppermute | solution.py:40
  148.0 2.5 %collective-permute-done.16 = bf16[512,256]{1,0:T(8,128)(2,1)S(1)} collective-permute-done((bf16[512,256]{1,0:T(8,128)(2,1)S(1)}, bf16[512,256]{1,0:T(8,128)(2,1)S(1)}, u32[]{:S(2)}, u32[]{:S(2)}) %collective-permute-start.16) | collective-permute-done | bytes 262176 | tf_op jit(solution)/shard_map/ppermute | solution.py:40
  150.4 11.2 %collective-permute-done.17 = bf16[512,256]{1,0:T(8,128)(2,1)S(1)} collective-permute-done((bf16[512,256]{1,0:T(8,128)(2,1)S(1)}, bf16[512,256]{1,0:T(8,128)(2,1)S(1)}, u32[]{:S(2)}, u32[]{:S(2)}) %collective-permute-start.17) | collective-permute-done | bytes 262176 | tf_op jit(solution)/shard_map/ppermute | solution.py:40
  163.7 5.7 %collective-permute-done.14 = bf16[256,256]{1,0:T(8,128)(2,1)S(1)} collective-permute-done((bf16[256,256]{1,0:T(8,128)(2,1)S(1)}, bf16[256,256]{1,0:T(8,128)(2,1)S(1)}, u32[]{:S(2)}, u32[]{:S(2)}) %collective-permute-start.14) | collective-permute-done | bytes 131104 | tf_op jit(solution)/shard_map/ppermute | solution.py:40
  169.4 16.7 %collective-permute-done.18 = bf16[256,256]{1,0:T(8,128)(2,1)S(1)} collective-permute-done((bf16[256,256]{1,0:T(8,128)(2,1)S(1)}, bf16[256,256]{1,0:T(8,128)(2,1)S(1)}, u32[]{:S(2)}, u32[]{:S(2)}) %collective-permute-start.18) | collective-permute-done | bytes 131104 | tf_op jit(solution)/shard_map/ppermute | solution.py:40
  (53 shorter events, 15.9 us)
Async XLA Ops:
  1.3 19.4 %copy-start.5 = (bf16[1,128,512]{2,1,0:T(8,128)(2,1)S(1)}, bf16[1,128,512]{2,1,0:T(8,128)(2,1)}, u32[]{:S(2)}) copy-start(bf16[1,128,512]{2,1,0:T(8,128)(2,1)} %param.8) | copy-start | bytes 393220
  2.3 62.8 %copy-start = (bf16[1,128,2048]{2,1,0:T(8,128)(2,1)S(1)}, bf16[1,128,2048]{2,1,0:T(8,128)(2,1)}, u32[]{:S(2)}) copy-start(bf16[1,128,2048]{2,1,0:T(8,128)(2,1)} %param.7) | copy-start | bytes 1572868
  2.3 62.8 %copy-start.1 = (bf16[1,128,2048]{2,1,0:T(8,128)(2,1)S(1)}, bf16[1,128,2048]{2,1,0:T(8,128)(2,1)}, u32[]{:S(2)}) copy-start(bf16[1,128,2048]{2,1,0:T(8,128)(2,1)} %param.10) | copy-start | bytes 1572868
  2.4 29.9 %collective-permute-start.7 = (bf16[264,256]{1,0:T(8,128)(2,1)S(1)}, bf16[264,256]{1,0:T(8,128)(2,1)S(1)}, u32[]{:S(2)}, u32[]{:S(2)}) collective-permute-start(bf16[264,256]{1,0:T(8,128)(2,1)S(1)} %get-tuple-element.43), channel_id=1, source_target_pairs={{0,1},{1,2},{2,3},{3,4},{4,5},{5,6},{6,7},{7,8},{8,9},{9,10},{10,1... | collective-permute-start | bytes 405512 | tf_op jit(solution)/shard_map/ppermute | solution.py:40
  20.8 44.3 %copy-start.6 = (f32[16]{0:T(128)S(1)}, f32[16]{0:T(128)}, u32[]{:S(2)}) copy-start(f32[16]{0:T(128)} %param.11) | copy-start | bytes 196
  20.8 42.3 %collective-permute-start.1 = (bf16[264,512]{1,0:T(8,128)(2,1)S(1)}, bf16[264,512]{1,0:T(8,128)(2,1)S(1)}, u32[]{:S(2)}, u32[]{:S(2)}) collective-permute-start(bf16[264,512]{1,0:T(8,128)(2,1)S(1)} %pad_maximum_fusion.refs_0_), channel_id=1, source_target_pairs={{0,2},{1,3},{2,4},{3,5},{4,6},{5,7},{6,8},{7,9},{8,10},{9,11},{10,... | collective-permute-start | bytes 811016 | tf_op jit(solution)/shard_map/ppermute | solution.py:40
  25.1 19.4 %collective-permute-start = (bf16[264,256]{1,0:T(8,128)(2,1)S(1)}, bf16[264,256]{1,0:T(8,128)(2,1)S(1)}, u32[]{:S(2)}, u32[]{:S(2)}) collective-permute-start(bf16[264,256]{1,0:T(8,128)(2,1)S(1)} %get-tuple-element.44), channel_id=1, source_target_pairs={{0,1},{1,2},{2,3},{3,4},{4,5},{5,6},{6,7},{7,8},{8,9},{9,10},{10,1... | collective-permute-start | bytes 405512 | tf_op jit(solution)/shard_map/ppermute | solution.py:40
  32.3 15.9 %collective-permute-start.10 = (bf16[264,256]{1,0:T(8,128)(2,1)S(1)}, bf16[264,256]{1,0:T(8,128)(2,1)S(1)}, u32[]{:S(2)}, u32[]{:S(2)}) collective-permute-start(bf16[264,256]{1,0:T(8,128)(2,1)S(1)} %collective-permute-done.7.refs_1_), channel_id=1, source_target_pairs={{0,6},{1,7},{2,8},{3,9},{4,10},{5,11},{6,12},{7,13},{8,14},{9,15},... | collective-permute-start | bytes 405512 | tf_op jit(solution)/shard_map/ppermute | solution.py:40
  36.7 13.5 %collective-permute-start.8 = (bf16[264,256]{1,0:T(8,128)(2,1)S(1)}, bf16[264,256]{1,0:T(8,128)(2,1)S(1)}, u32[]{:S(2)}, u32[]{:S(2)}) collective-permute-start(bf16[264,256]{1,0:T(8,128)(2,1)S(1)} %collective-permute-done.7.refs_1_), channel_id=1, source_target_pairs={{0,2},{1,3},{2,4},{3,5},{4,6},{5,7},{6,8},{7,9},{8,10},{9,11},{10,... | collective-permute-start | bytes 405512 | tf_op jit(solution)/shard_map/ppermute | solution.py:40
  41.0 20.1 %collective-permute-start.9 = (bf16[264,256]{1,0:T(8,128)(2,1)S(1)}, bf16[264,256]{1,0:T(8,128)(2,1)S(1)}, u32[]{:S(2)}, u32[]{:S(2)}) collective-permute-start(bf16[264,256]{1,0:T(8,128)(2,1)S(1)} %collective-permute-done.7.refs_1_), channel_id=1, source_target_pairs={{0,4},{1,5},{2,6},{3,7},{4,8},{5,9},{6,10},{7,11},{8,12},{9,13},{1... | collective-permute-start | bytes 405512 | tf_op jit(solution)/shard_map/ppermute | solution.py:40
  44.5 20.6 %collective-permute-start.3 = (bf16[264,512]{1,0:T(8,128)(2,1)S(1)}, bf16[264,512]{1,0:T(8,128)(2,1)S(1)}, u32[]{:S(2)}, u32[]{:S(2)}) collective-permute-start(bf16[264,512]{1,0:T(8,128)(2,1)S(1)} %pad_maximum_fusion.refs_0_), channel_id=1, source_target_pairs={{0,4},{1,5},{2,6},{3,7},{4,8},{5,9},{6,10},{7,11},{8,12},{9,13},{1... | collective-permute-start | bytes 811016 | tf_op jit(solution)/shard_map/ppermute | solution.py:40
  48.2 16.9 %collective-permute-start.5 = (bf16[264,512]{1,0:T(8,128)(2,1)S(1)}, bf16[264,512]{1,0:T(8,128)(2,1)S(1)}, u32[]{:S(2)}, u32[]{:S(2)}) collective-permute-start(bf16[264,512]{1,0:T(8,128)(2,1)S(1)} %pad_maximum_fusion.refs_0_), channel_id=1, source_target_pairs={{0,6},{1,7},{2,8},{3,9},{4,10},{5,11},{6,12},{7,13},{8,14},{9,15},... | collective-permute-start | bytes 811016 | tf_op jit(solution)/shard_map/ppermute | solution.py:40
  50.2 22.9 %collective-permute-start.2 = (bf16[264,256]{1,0:T(8,128)(2,1)S(1)}, bf16[264,256]{1,0:T(8,128)(2,1)S(1)}, u32[]{:S(2)}, u32[]{:S(2)}) collective-permute-start(bf16[264,256]{1,0:T(8,128)(2,1)S(1)} %collective-permute-done.refs_1_), channel_id=1, source_target_pairs={{0,2},{1,3},{2,4},{3,5},{4,6},{5,7},{6,8},{7,9},{8,10},{9,11},{10,... | collective-permute-start | bytes 405512 | tf_op jit(solution)/shard_map/ppermute | solution.py:40
  61.2 11.8 %collective-permute-start.4 = (bf16[264,256]{1,0:T(8,128)(2,1)S(1)}, bf16[264,256]{1,0:T(8,128)(2,1)S(1)}, u32[]{:S(2)}, u32[]{:S(2)}) collective-permute-start(bf16[264,256]{1,0:T(8,128)(2,1)S(1)} %collective-permute-done.refs_1_), channel_id=1, source_target_pairs={{0,4},{1,5},{2,6},{3,7},{4,8},{5,9},{6,10},{7,11},{8,12},{9,13},{1... | collective-permute-start | bytes 405512 | tf_op jit(solution)/shard_map/ppermute | solution.py:40
  63.1 9.9 %collective-permute-start.6 = (bf16[264,256]{1,0:T(8,128)(2,1)S(1)}, bf16[264,256]{1,0:T(8,128)(2,1)S(1)}, u32[]{:S(2)}, u32[]{:S(2)}) collective-permute-start(bf16[264,256]{1,0:T(8,128)(2,1)S(1)} %collective-permute-done.refs_1_), channel_id=1, source_target_pairs={{0,6},{1,7},{2,8},{3,9},{4,10},{5,11},{6,12},{7,13},{8,14},{9,15},... | collective-permute-start | bytes 405512 | tf_op jit(solution)/shard_map/ppermute | solution.py:40
  105.6 30.1 %all-to-all-start.1 = ((f32[64,1,128]{2,1,0:T(1,128)}), f32[64,1,128]{2,1,0:T(1,128)S(1)}, u32[]{:S(2)}, u32[]{:S(2)}) async-start(f32[64,1,128]{2,1,0:T(1,128)} %broadcast_in_dim.38), calls=%async_computation.1 | async-start | bytes 65536 | tf_op jit(solution)/shard_map/all_to_all | solution.py:231
  121.1 15.1 %collective-permute-start.11 = (bf16[512,256]{1,0:T(8,128)(2,1)S(1)}, bf16[512,256]{1,0:T(8,128)(2,1)S(1)}, u32[]{:S(2)}, u32[]{:S(2)}) collective-permute-start(bf16[512,256]{1,0:T(8,128)(2,1)S(1)} %get-tuple-element.29), channel_id=1, source_target_pairs={{6,0},{7,1},{8,2},{9,3},{10,4},{11,5},{12,6},{13,7},{14,8},{15,9},... | collective-permute-start | bytes 786440 | tf_op jit(solution)/shard_map/ppermute | solution.py:40
  123.3 16.2 %collective-permute-start.12 = (bf16[512,256]{1,0:T(8,128)(2,1)S(1)}, bf16[512,256]{1,0:T(8,128)(2,1)}, u32[]{:S(2)}, u32[]{:S(2)}) collective-permute-start(bf16[512,256]{1,0:T(8,128)(2,1)S(1)} %get-tuple-element.30), channel_id=1, source_target_pairs={{4,0},{5,1},{6,2},{7,3},{8,4},{9,5},{10,6},{11,7},{12,8},{13,9},{1... | collective-permute-start | bytes 786440 | tf_op jit(solution)/shard_map/ppermute | solution.py:40
  127.2 17.6 %collective-permute-start.13 = (bf16[512,256]{1,0:T(8,128)(2,1)S(1)}, bf16[512,256]{1,0:T(8,128)(2,1)}, u32[]{:S(2)}, u32[]{:S(2)}) collective-permute-start(bf16[512,256]{1,0:T(8,128)(2,1)S(1)} %get-tuple-element.31), channel_id=1, source_target_pairs={{2,0},{3,1},{4,2},{5,3},{6,4},{7,5},{8,6},{9,7},{10,8},{11,9},{12,... | collective-permute-start | bytes 786440 | tf_op jit(solution)/shard_map/ppermute | solution.py:40
  129.2 18.8 %collective-permute-start.15 = (bf16[512,256]{1,0:T(8,128)(2,1)S(1)}, bf16[512,256]{1,0:T(8,128)(2,1)S(1)}, u32[]{:S(2)}, u32[]{:S(2)}) collective-permute-start(bf16[512,256]{1,0:T(8,128)(2,1)S(1)} %get-tuple-element.33), channel_id=1, source_target_pairs={{6,0},{7,1},{8,2},{9,3},{10,4},{11,5},{12,6},{13,7},{14,8},{15,9},... | collective-permute-start | bytes 786440 | tf_op jit(solution)/shard_map/ppermute | solution.py:40
  133.7 16.7 %collective-permute-start.16 = (bf16[512,256]{1,0:T(8,128)(2,1)S(1)}, bf16[512,256]{1,0:T(8,128)(2,1)S(1)}, u32[]{:S(2)}, u32[]{:S(2)}) collective-permute-start(bf16[512,256]{1,0:T(8,128)(2,1)S(1)} %get-tuple-element.34), channel_id=1, source_target_pairs={{4,0},{5,1},{6,2},{7,3},{8,4},{9,5},{10,6},{11,7},{12,8},{13,9},{1... | collective-permute-start | bytes 786440 | tf_op jit(solution)/shard_map/ppermute | solution.py:40
  136.2 25.4 %collective-permute-start.17 = (bf16[512,256]{1,0:T(8,128)(2,1)S(1)}, bf16[512,256]{1,0:T(8,128)(2,1)S(1)}, u32[]{:S(2)}, u32[]{:S(2)}) collective-permute-start(bf16[512,256]{1,0:T(8,128)(2,1)S(1)} %get-tuple-element.35), channel_id=1, source_target_pairs={{2,0},{3,1},{4,2},{5,3},{6,4},{7,5},{8,6},{9,7},{10,8},{11,9},{12,... | collective-permute-start | bytes 786440 | tf_op jit(solution)/shard_map/ppermute | solution.py:40
  146.0 23.4 %collective-permute-start.14 = (bf16[256,256]{1,0:T(8,128)(2,1)S(1)}, bf16[256,256]{1,0:T(8,128)(2,1)S(1)}, u32[]{:S(2)}, u32[]{:S(2)}) collective-permute-start(bf16[256,256]{1,0:T(8,128)(2,1)S(1)} %slice.95), channel_id=1, source_target_pairs={{1,0},{2,1},{3,2},{4,3},{5,4},{6,5},{7,6},{8,7},{9,8},{10,9},{11,1... | collective-permute-start | bytes 393224 | tf_op jit(solution)/shard_map/ppermute | solution.py:40
  161.7 24.4 %collective-permute-start.18 = (bf16[256,256]{1,0:T(8,128)(2,1)S(1)}, bf16[256,256]{1,0:T(8,128)(2,1)S(1)}, u32[]{:S(2)}, u32[]{:S(2)}) collective-permute-start(bf16[256,256]{1,0:T(8,128)(2,1)S(1)} %slice.94), channel_id=1, source_target_pairs={{1,0},{2,1},{3,2},{4,3},{5,4},{6,5},{7,6},{8,7},{9,8},{10,9},{11,1... | collective-permute-start | bytes 393224 | tf_op jit(solution)/shard_map/ppermute | solution.py:40
  (3 other events, 20.7 us)

commit v2 on v1

--- a/solution.py
+++ b/solution.py
@@ -56,8 +56,8 @@
     *refs,
 ):
     packs = refs[:MOST]
-    sink_in_ref = None if fresh else refs[MOST + 2]
-    refs = refs[MOST:] if fresh else refs[MOST + 3 :]
+    sink_in_ref = None if fresh else refs[MOST + 6]
+    refs = refs[MOST:] if fresh else refs[MOST + 7 :]
     (out_ref, grad_query_ref, near_ref, far2_ref, far4_ref, far6_ref, sink_grad_ref) = refs[:7]
     mask_ref, score_ref, cross_ref, weight_ref, slope_ref = refs[7:]
     step = pl.program_id(0)
@@ -169,9 +169,9 @@
     wide = pl.BlockSpec((TOK, GROUP_COLS), lambda h: (0, first + h))
     whole_pack = pl.BlockSpec((PACK_ROWS, HEAD_DIM), lambda h: (0, first + h))
     chunk_pack = pl.BlockSpec((PACK_ROWS, HEAD_DIM), lambda h: (0, h))
-    pair_spec = pl.BlockSpec((4 * TOK, HEAD_DIM), lambda h: (0, h))
+    pair_spec = pl.BlockSpec((4 * TOK, HEAD_DIM), lambda h: (0, first + h))
     smem = pl.BlockSpec(memory_space=pltpu.SMEM)
-    pair_shape = (4 * TOK, CHUNK_COLS)
+    pair_shape = (4 * TOK, KV_COLS)
     heads = CHUNK_HEADS * GROUP
     sink_spec = pl.BlockSpec((Z_MEMBERS, TOK), lambda h: (0, 0))
     n_fixed = 6 + MOST
@@ -180,7 +180,7 @@
         grid=(CHUNK_HEADS,),
         in_specs=[smem, smem, smem, pl.BlockSpec((1, TOK), lambda h: (0, 0)), wide, wide]
         + [chunk_pack if pack.shape[1] == CHUNK_COLS else whole_pack for pack in packs]
-        + ([pl.BlockSpec(memory_space=pl.ANY)] * 2 + [sink_spec] if written else []),
+        + ([pl.BlockSpec(memory_space=pl.ANY)] * 6 + [sink_spec] if written else []),
         out_specs=[
             wide,
             wide,
@@ -206,7 +206,7 @@
             pltpu.VMEM((WIN, GROUP_COLS), jnp.bfloat16),
             pltpu.VMEM((WIN, GROUP_COLS), jnp.bfloat16),
         ],
-        input_output_aliases={n_fixed: 0, n_fixed + 1: 1} if written else {},
+        input_output_aliases={n_fixed + out: out for out in range(6)} if written else {},
         compiler_params=pltpu.CompilerParams(
             dimension_semantics=("arbitrary",), vmem_limit_bytes=20 << 20
         ),
@@ -252,15 +252,12 @@
     for by in (6, 4, 2):
         evens[by] = passed_along(own, by)
     outs = ()
-    sinks = ()
-    kept = []
-    returned = []
     for chunk in range(CHUNKS):
         odds = {1: near_odd[chunk]}
         for by in (6, 4, 2):
             odds[by + 1] = passed_along(near_odd[chunk], by)
         packs = [(odds if slot % 2 else evens)[slot] for slot in range(MOST)]
-        *outs, near, far2, far4, far6, sinks = attention(
+        outs = attention(
             chunk,
             place,
             run_lengths[0],
@@ -269,23 +266,18 @@
             queries[0],
             cotangent[0],
             packs,
-            (*outs, sinks) if outs else (),
+            tuple(outs),
         )
-        kept.append(near)
-        back = []
-        for by, far in ((6, far6), (4, far4), (2, far2)):
-            back.append(passed_along(far, -by))
-        returned.append(back)
-    attended, grad_query = outs
+    attended, grad_query, near, far2, far4, far6, sinks = outs
+    returned = []
+    for by, far in ((6, far6), (4, far4), (2, far2)):
+        returned.append(passed_along(far, -by))
     grad_sink = exchanged(sinks, ("ctx_2", "dp_0"))
-    grad_kv = []
-    for chunk in range(CHUNKS):
-        near = kept[chunk] + sum(part.astype(jnp.float32) for part in returned[chunk])
-        last = passed_along(near[2 * TOK :].astype(jnp.bfloat16), -1)
-        grad_kv.append((near[: 2 * TOK] + last.astype(jnp.float32)).astype(jnp.bfloat16))
+    near = near + sum(part.astype(jnp.float32) for part in returned)
+    last = passed_along(near[2 * TOK :].astype(jnp.bfloat16), -1)
+    grad_kv = (near[: 2 * TOK] + last.astype(jnp.float32)).astype(jnp.bfloat16)
     spread = jnp.broadcast_to(grad_sink[None], (PLANE_MEMBERS, TOK))
     grad_sink = exchanged(spread, ("ctx_0", "ctx_1", "dp_1"))[:HEADS]
-    grad_kv = jnp.concatenate(grad_kv, axis=1)
     scale_down = 1.0 / math.sqrt(lax.axis_size(DP) * n_ctx * TOK)
     return (
         attended[None],

time: 188 us -> 169 us (0.90)
  the two profiles are of different devices: /device:TPU:95 before, /device:TPU:104 now
where the time goes in v2:
time: 169 us; the launch traced here: 168 us
  starting transfers between devices  79.3 us (47%)
  waiting for transfers between devices  44.8 us (27%)
  blocking collectives  22.8 us (13%)
  Pallas kernels  14.6 us (9%)
  local copies, waits for them, and re-layouts  3.8 us (2%)
  other arithmetic  2.15 us (1%)
    ppermute x15, starting transfers between devices, passed_along(): return lax.ppermute(array, CTX, pairs)  69.9 us
    ppermute x15, waiting for transfers between devices, passed_along(): return lax.ppermute(array, CTX, pairs)  44.8 us
    all_to_all x1, blocking collectives, exchanged(): return jnp.sum(lax.all_to_all(spread, axes, 0, 0, tiled=True), axis=0)  22.8 us
    pallas_call x2, Pallas kernels, attention(): pl.pallas_call(functools.partial(attention_kernel, not written, first * G...  14.6 us
    all_to_all x1, starting transfers between devices, exchanged(): return jnp.sum(lax.all_to_all(spread, axes, 0, 0, tiled=True), axis=0)  9.37 us
  transfers between devices with their start and end apart: 16, of which 4 were waited for; matrix products, arithmetic and copies ran while one was open for 2% of the time, Pallas kernels for 4%

profile of v2, /device:TPU:104, one launch (start us, length us, event | category | flops | bytes accessed | tf_op | source)
XLA Modules:
  0.0 168.4 jit_solution(7177088177086554851)
XLA Ops:
  1.3 1.0 fusion.1
  2.4 18.6 %collective-permute-start.7 = (bf16[264,256]{1,0:T(8,128)(2,1)S(1)}, bf16[264,256]{1,0:T(8,128)(2,1)S(1)}, u32[]{:S(2)}, u32[]{:S(2)}) collective-permute-start(bf16[264,256]{1,0:T(8,128)(2,1)S(1)} %get-tuple-element.43), channel_id=1, source_target_pairs={{0,1},{1,2},{2,3},{3,4},{4,5},{5,6},{6,7},{7,8},{8,9},{9,10},{10,1... | collective-permute-start | bytes 405512 | tf_op jit(solution)/shard_map/ppermute | solution.py:40
  21.1 4.7 %collective-permute-start.5 = (bf16[264,512]{1,0:T(8,128)(2,1)S(1)}, bf16[264,512]{1,0:T(8,128)(2,1)S(1)}, u32[]{:S(2)}, u32[]{:S(2)}) collective-permute-start(bf16[264,512]{1,0:T(8,128)(2,1)S(1)} %pad_maximum_fusion.refs_0_), channel_id=1, source_target_pairs={{0,6},{1,7},{2,8},{3,9},{4,10},{5,11},{6,12},{7,13},{8,14},{9,15},... | collective-permute-start | bytes 811016 | tf_op jit(solution)/shard_map/ppermute | solution.py:40
  25.7 1.9 %collective-permute-start = (bf16[264,256]{1,0:T(8,128)(2,1)S(1)}, bf16[264,256]{1,0:T(8,128)(2,1)S(1)}, u32[]{:S(2)}, u32[]{:S(2)}) collective-permute-start(bf16[264,256]{1,0:T(8,128)(2,1)S(1)} %get-tuple-element.44), channel_id=1, source_target_pairs={{0,1},{1,2},{2,3},{3,4},{4,5},{5,6},{6,7},{7,8},{8,9},{9,10},{10,1... | collective-permute-start | bytes 405512 | tf_op jit(solution)/shard_map/ppermute | solution.py:40
  27.7 9.7 %collective-permute-done.7.refs_1_ = bf16[264,256]{1,0:T(8,128)(2,1)S(1)} collective-permute-done((bf16[264,256]{1,0:T(8,128)(2,1)S(1)}, bf16[264,256]{1,0:T(8,128)(2,1)S(1)}, u32[]{:S(2)}, u32[]{:S(2)}) %collective-permute-start.7) | collective-permute-done | bytes 135200 | tf_op jit(solution)/shard_map/ppermute | solution.py:40
  37.3 5.8 %collective-permute-start.10 = (bf16[264,256]{1,0:T(8,128)(2,1)S(1)}, bf16[264,256]{1,0:T(8,128)(2,1)S(1)}, u32[]{:S(2)}, u32[]{:S(2)}) collective-permute-start(bf16[264,256]{1,0:T(8,128)(2,1)S(1)} %collective-permute-done.7.refs_1_), channel_id=1, source_target_pairs={{0,6},{1,7},{2,8},{3,9},{4,10},{5,11},{6,12},{7,13},{8,14},{9,15},... | collective-permute-start | bytes 405512 | tf_op jit(solution)/shard_map/ppermute | solution.py:40
  43.1 1.9 %collective-permute-start.9 = (bf16[264,256]{1,0:T(8,128)(2,1)S(1)}, bf16[264,256]{1,0:T(8,128)(2,1)S(1)}, u32[]{:S(2)}, u32[]{:S(2)}) collective-permute-start(bf16[264,256]{1,0:T(8,128)(2,1)S(1)} %collective-permute-done.7.refs_1_), channel_id=1, source_target_pairs={{0,4},{1,5},{2,6},{3,7},{4,8},{5,9},{6,10},{7,11},{8,12},{9,13},{1... | collective-permute-start | bytes 405512 | tf_op jit(solution)/shard_map/ppermute | solution.py:40
  45.1 2.8 %collective-permute-start.8 = (bf16[264,256]{1,0:T(8,128)(2,1)S(1)}, bf16[264,256]{1,0:T(8,128)(2,1)S(1)}, u32[]{:S(2)}, u32[]{:S(2)}) collective-permute-start(bf16[264,256]{1,0:T(8,128)(2,1)S(1)} %collective-permute-done.7.refs_1_), channel_id=1, source_target_pairs={{0,2},{1,3},{2,4},{3,5},{4,6},{5,7},{6,8},{7,9},{8,10},{9,11},{10,... | collective-permute-start | bytes 405512 | tf_op jit(solution)/shard_map/ppermute | solution.py:40
  47.9 4.7 %collective-permute-done.refs_1_ = bf16[264,256]{1,0:T(8,128)(2,1)S(1)} collective-permute-done((bf16[264,256]{1,0:T(8,128)(2,1)S(1)}, bf16[264,256]{1,0:T(8,128)(2,1)S(1)}, u32[]{:S(2)}, u32[]{:S(2)}) %collective-permute-start) | collective-permute-done | bytes 135200 | tf_op jit(solution)/shard_map/ppermute | solution.py:40
  52.6 1.9 %collective-permute-start.3 = (bf16[264,512]{1,0:T(8,128)(2,1)S(1)}, bf16[264,512]{1,0:T(8,128)(2,1)S(1)}, u32[]{:S(2)}, u32[]{:S(2)}) collective-permute-start(bf16[264,512]{1,0:T(8,128)(2,1)S(1)} %pad_maximum_fusion.refs_0_), channel_id=1, source_target_pairs={{0,4},{1,5},{2,6},{3,7},{4,8},{5,9},{6,10},{7,11},{8,12},{9,13},{1... | collective-permute-start | bytes 811016 | tf_op jit(solution)/shard_map/ppermute | solution.py:40
  54.5 1.9 %collective-permute-start.1 = (bf16[264,512]{1,0:T(8,128)(2,1)S(1)}, bf16[264,512]{1,0:T(8,128)(2,1)S(1)}, u32[]{:S(2)}, u32[]{:S(2)}) collective-permute-start(bf16[264,512]{1,0:T(8,128)(2,1)S(1)} %pad_maximum_fusion.refs_0_), channel_id=1, source_target_pairs={{0,2},{1,3},{2,4},{3,5},{4,6},{5,7},{6,8},{7,9},{8,10},{9,11},{10,... | collective-permute-start | bytes 811016 | tf_op jit(solution)/shard_map/ppermute | solution.py:40
  56.5 7.0 %collective-permute-start.6 = (bf16[264,256]{1,0:T(8,128)(2,1)S(1)}, bf16[264,256]{1,0:T(8,128)(2,1)S(1)}, u32[]{:S(2)}, u32[]{:S(2)}) collective-permute-start(bf16[264,256]{1,0:T(8,128)(2,1)S(1)} %collective-permute-done.refs_1_), channel_id=1, source_target_pairs={{0,6},{1,7},{2,8},{3,9},{4,10},{5,11},{6,12},{7,13},{8,14},{9,15},... | collective-permute-start | bytes 405512 | tf_op jit(solution)/shard_map/ppermute | solution.py:40
  63.5 2.8 %collective-permute-start.4 = (bf16[264,256]{1,0:T(8,128)(2,1)S(1)}, bf16[264,256]{1,0:T(8,128)(2,1)S(1)}, u32[]{:S(2)}, u32[]{:S(2)}) collective-permute-start(bf16[264,256]{1,0:T(8,128)(2,1)S(1)} %collective-permute-done.refs_1_), channel_id=1, source_target_pairs={{0,4},{1,5},{2,6},{3,7},{4,8},{5,9},{6,10},{7,11},{8,12},{9,13},{1... | collective-permute-start | bytes 405512 | tf_op jit(solution)/shard_map/ppermute | solution.py:40
  66.2 1.9 %collective-permute-start.2 = (bf16[264,256]{1,0:T(8,128)(2,1)S(1)}, bf16[264,256]{1,0:T(8,128)(2,1)S(1)}, u32[]{:S(2)}, u32[]{:S(2)}) collective-permute-start(bf16[264,256]{1,0:T(8,128)(2,1)S(1)} %collective-permute-done.refs_1_), channel_id=1, source_target_pairs={{0,2},{1,3},{2,4},{3,5},{4,6},{5,7},{6,8},{7,9},{8,10},{9,11},{10,... | collective-permute-start | bytes 405512 | tf_op jit(solution)/shard_map/ppermute | solution.py:40
  69.8 7.2 %shard_map.110 = (bf16[128,2048]{1,0:T(8,128)(2,1)}, bf16[128,2048]{1,0:T(8,128)(2,1)}, f32[512,512]{1,0:T(8,128)S(1)}, bf16[512,512]{1,0:T(8,128)(2,1)S(1)}, bf...) custom-call(s32[1]{0:T(128)} %bitcast.place_ref, s32[16]{0:T(128)S(1)} %bitcast.27, ...), custom_call_target="tpu_custom_call" | custom-call | flops 1342177280 | bytes 4194304 | tf_op jit(solution)/shard_map/pallas_call | solution.py:178
  77.1 7.3 %shard_map.111 = (bf16[128,2048]{1,0:T(8,128)(2,1)}, bf16[128,2048]{1,0:T(8,128)(2,1)}, f32[512,512]{1,0:T(8,128)S(1)}, bf16[512,512]{1,0:T(8,128)(2,1)S(1)}, bf...) custom-call(s32[1]{0:T(128)} %bitcast.place_ref, ...), custom_call_target="tpu_custom_call", output_to_operand_aliasing={{0}: (14, {}), {1}: (15, {}), {2}: (16, {}), {3}: (17, {}),... | custom-call | flops 1342177280 | bytes 4194304 | tf_op jit(solution)/shard_map/pallas_call | solution.py:178
  84.4 4.5 %collective-permute-start.11 = (bf16[512,512]{1,0:T(8,128)(2,1)S(1)}, bf16[512,512]{1,0:T(8,128)(2,1)S(1)}, u32[]{:S(2)}, u32[]{:S(2)}) collective-permute-start(bf16[512,512]{1,0:T(8,128)(2,1)S(1)} %get-tuple-element.33), channel_id=1, source_target_pairs={{6,0},{7,1},{8,2},{9,3},{10,4},{11,5},{12,6},{13,7},{14,8},{15,9},... | collective-permute-start | bytes 1572872 | tf_op jit(solution)/shard_map/ppermute | solution.py:40
  88.9 5.8 %collective-permute-start.12 = (bf16[512,512]{1,0:T(8,128)(2,1)S(1)}, bf16[512,512]{1,0:T(8,128)(2,1)}, u32[]{:S(2)}, u32[]{:S(2)}) collective-permute-start(bf16[512,512]{1,0:T(8,128)(2,1)S(1)} %get-tuple-element.34), channel_id=1, source_target_pairs={{4,0},{5,1},{6,2},{7,3},{8,4},{9,5},{10,6},{11,7},{12,8},{13,9},{1... | collective-permute-start | bytes 1572872 | tf_op jit(solution)/shard_map/ppermute | solution.py:40
  94.7 2.1 %collective-permute-start.13 = (bf16[512,512]{1,0:T(8,128)(2,1)S(1)}, bf16[512,512]{1,0:T(8,128)(2,1)}, u32[]{:S(2)}, u32[]{:S(2)}) collective-permute-start(bf16[512,512]{1,0:T(8,128)(2,1)S(1)} %get-tuple-element.35), channel_id=1, source_target_pairs={{2,0},{3,1},{4,2},{5,3},{6,4},{7,5},{8,6},{9,7},{10,8},{11,9},{12,... | collective-permute-start | bytes 1572872 | tf_op jit(solution)/shard_map/ppermute | solution.py:40
  96.8 22.8 %all_to_all.15 = f32[16,1,128]{2,1,0:T(1,128)S(1)} all-to-all(f32[16,1,128]{2,1,0:T(1,128)S(1)} %bitcast.26), channel_id=1, replica_groups=mesh['dp_0'=8,'dp_1'=2,'ctx_0'=8,'ctx_1'=4,'ctx_2'=2] {'ctx_2','dp_0'}, dimensions={0} | all-to-all | bytes 16384 | tf_op jit(solution)/shard_map/all_to_all | solution.py:231
  120.3 9.4 %all-to-all-start.1 = ((f32[64,1,128]{2,1,0:T(1,128)}), f32[64,1,128]{2,1,0:T(1,128)S(1)}, u32[]{:S(2)}, u32[]{:S(2)}) async-start(f32[64,1,128]{2,1,0:T(1,128)} %broadcast_in_dim.38), calls=%async_computation.1 | async-start | bytes 65536 | tf_op jit(solution)/shard_map/all_to_all | solution.py:231
  129.7 1.5 add_add_fusion
  131.2 6.4 %collective-permute-start.14 = (bf16[256,512]{1,0:T(8,128)(2,1)S(1)}, bf16[256,512]{1,0:T(8,128)(2,1)S(1)}, u32[]{:S(2)}, u32[]{:S(2)}) collective-permute-start(bf16[256,512]{1,0:T(8,128)(2,1)S(1)} %slice.73), channel_id=1, source_target_pairs={{1,0},{2,1},{3,2},{4,3},{5,4},{6,5},{7,6},{8,7},{9,8},{10,9},{11,1... | collective-permute-start | bytes 786440 | tf_op jit(solution)/shard_map/ppermute | solution.py:40
  138.2 29.4 %collective-permute-done.14 = bf16[256,512]{1,0:T(8,128)(2,1)S(1)} collective-permute-done((bf16[256,512]{1,0:T(8,128)(2,1)S(1)}, bf16[256,512]{1,0:T(8,128)(2,1)S(1)}, u32[]{:S(2)}, u32[]{:S(2)}) %collective-permute-start.14) | collective-permute-done | bytes 262176 | tf_op jit(solution)/shard_map/ppermute | solution.py:40
  (42 shorter events, 4.5 us)
Async XLA Ops:
  0.6 0.7 copy-start.3
  1.3 19.7 %copy-start.4 = (bf16[1,128,512]{2,1,0:T(8,128)(2,1)S(1)}, bf16[1,128,512]{2,1,0:T(8,128)(2,1)}, u32[]{:S(2)}) copy-start(bf16[1,128,512]{2,1,0:T(8,128)(2,1)} %param.9) | copy-start | bytes 393220
  1.3 19.7 %copy-start.5 = (bf16[1,128,512]{2,1,0:T(8,128)(2,1)S(1)}, bf16[1,128,512]{2,1,0:T(8,128)(2,1)}, u32[]{:S(2)}) copy-start(bf16[1,128,512]{2,1,0:T(8,128)(2,1)} %param.8) | copy-start | bytes 393220
  2.3 66.9 %copy-start = (bf16[1,128,2048]{2,1,0:T(8,128)(2,1)S(1)}, bf16[1,128,2048]{2,1,0:T(8,128)(2,1)}, u32[]{:S(2)}) copy-start(bf16[1,128,2048]{2,1,0:T(8,128)(2,1)} %param.7) | copy-start | bytes 1572868
  2.3 66.8 %copy-start.1 = (bf16[1,128,2048]{2,1,0:T(8,128)(2,1)S(1)}, bf16[1,128,2048]{2,1,0:T(8,128)(2,1)}, u32[]{:S(2)}) copy-start(bf16[1,128,2048]{2,1,0:T(8,128)(2,1)} %param.10) | copy-start | bytes 1572868
  2.4 35.0 %collective-permute-start.7 = (bf16[264,256]{1,0:T(8,128)(2,1)S(1)}, bf16[264,256]{1,0:T(8,128)(2,1)S(1)}, u32[]{:S(2)}, u32[]{:S(2)}) collective-permute-start(bf16[264,256]{1,0:T(8,128)(2,1)S(1)} %get-tuple-element.43), channel_id=1, source_target_pairs={{0,1},{1,2},{2,3},{3,4},{4,5},{5,6},{6,7},{7,8},{8,9},{9,10},{10,1... | collective-permute-start | bytes 405512 | tf_op jit(solution)/shard_map/ppermute | solution.py:40
  21.1 47.1 %copy-start.6 = (f32[16]{0:T(128)S(1)}, f32[16]{0:T(128)}, u32[]{:S(2)}) copy-start(f32[16]{0:T(128)} %param.11) | copy-start | bytes 196
  21.1 45.2 %collective-permute-start.5 = (bf16[264,512]{1,0:T(8,128)(2,1)S(1)}, bf16[264,512]{1,0:T(8,128)(2,1)S(1)}, u32[]{:S(2)}, u32[]{:S(2)}) collective-permute-start(bf16[264,512]{1,0:T(8,128)(2,1)S(1)} %pad_maximum_fusion.refs_0_), channel_id=1, source_target_pairs={{0,6},{1,7},{2,8},{3,9},{4,10},{5,11},{6,12},{7,13},{8,14},{9,15},... | collective-permute-start | bytes 811016 | tf_op jit(solution)/shard_map/ppermute | solution.py:40
  25.7 26.9 %collective-permute-start = (bf16[264,256]{1,0:T(8,128)(2,1)S(1)}, bf16[264,256]{1,0:T(8,128)(2,1)S(1)}, u32[]{:S(2)}, u32[]{:S(2)}) collective-permute-start(bf16[264,256]{1,0:T(8,128)(2,1)S(1)} %get-tuple-element.44), channel_id=1, source_target_pairs={{0,1},{1,2},{2,3},{3,4},{4,5},{5,6},{6,7},{7,8},{8,9},{9,10},{10,1... | collective-permute-start | bytes 405512 | tf_op jit(solution)/shard_map/ppermute | solution.py:40
  37.3 17.2 %collective-permute-start.10 = (bf16[264,256]{1,0:T(8,128)(2,1)S(1)}, bf16[264,256]{1,0:T(8,128)(2,1)S(1)}, u32[]{:S(2)}, u32[]{:S(2)}) collective-permute-start(bf16[264,256]{1,0:T(8,128)(2,1)S(1)} %collective-permute-done.7.refs_1_), channel_id=1, source_target_pairs={{0,6},{1,7},{2,8},{3,9},{4,10},{5,11},{6,12},{7,13},{8,14},{9,15},... | collective-permute-start | bytes 405512 | tf_op jit(solution)/shard_map/ppermute | solution.py:40
  43.1 13.3 %collective-permute-start.9 = (bf16[264,256]{1,0:T(8,128)(2,1)S(1)}, bf16[264,256]{1,0:T(8,128)(2,1)S(1)}, u32[]{:S(2)}, u32[]{:S(2)}) collective-permute-start(bf16[264,256]{1,0:T(8,128)(2,1)S(1)} %collective-permute-done.7.refs_1_), channel_id=1, source_target_pairs={{0,4},{1,5},{2,6},{3,7},{4,8},{5,9},{6,10},{7,11},{8,12},{9,13},{1... | collective-permute-start | bytes 405512 | tf_op jit(solution)/shard_map/ppermute | solution.py:40
  45.1 18.4 %collective-permute-start.8 = (bf16[264,256]{1,0:T(8,128)(2,1)S(1)}, bf16[264,256]{1,0:T(8,128)(2,1)S(1)}, u32[]{:S(2)}, u32[]{:S(2)}) collective-permute-start(bf16[264,256]{1,0:T(8,128)(2,1)S(1)} %collective-permute-done.7.refs_1_), channel_id=1, source_target_pairs={{0,2},{1,3},{2,4},{3,5},{4,6},{5,7},{6,8},{7,9},{8,10},{9,11},{10,... | collective-permute-start | bytes 405512 | tf_op jit(solution)/shard_map/ppermute | solution.py:40
  52.6 15.7 %collective-permute-start.3 = (bf16[264,512]{1,0:T(8,128)(2,1)S(1)}, bf16[264,512]{1,0:T(8,128)(2,1)S(1)}, u32[]{:S(2)}, u32[]{:S(2)}) collective-permute-start(bf16[264,512]{1,0:T(8,128)(2,1)S(1)} %pad_maximum_fusion.refs_0_), channel_id=1, source_target_pairs={{0,4},{1,5},{2,6},{3,7},{4,8},{5,9},{6,10},{7,11},{8,12},{9,13},{1... | collective-permute-start | bytes 811016 | tf_op jit(solution)/shard_map/ppermute | solution.py:40
  54.5 14.7 %collective-permute-start.1 = (bf16[264,512]{1,0:T(8,128)(2,1)S(1)}, bf16[264,512]{1,0:T(8,128)(2,1)S(1)}, u32[]{:S(2)}, u32[]{:S(2)}) collective-permute-start(bf16[264,512]{1,0:T(8,128)(2,1)S(1)} %pad_maximum_fusion.refs_0_), channel_id=1, source_target_pairs={{0,2},{1,3},{2,4},{3,5},{4,6},{5,7},{6,8},{7,9},{8,10},{9,11},{10,... | collective-permute-start | bytes 811016 | tf_op jit(solution)/shard_map/ppermute | solution.py:40
  56.5 20.6 %collective-permute-start.6 = (bf16[264,256]{1,0:T(8,128)(2,1)S(1)}, bf16[264,256]{1,0:T(8,128)(2,1)S(1)}, u32[]{:S(2)}, u32[]{:S(2)}) collective-permute-start(bf16[264,256]{1,0:T(8,128)(2,1)S(1)} %collective-permute-done.refs_1_), channel_id=1, source_target_pairs={{0,6},{1,7},{2,8},{3,9},{4,10},{5,11},{6,12},{7,13},{8,14},{9,15},... | collective-permute-start | bytes 405512 | tf_op jit(solution)/shard_map/ppermute | solution.py:40
  63.5 13.6 %collective-permute-start.4 = (bf16[264,256]{1,0:T(8,128)(2,1)S(1)}, bf16[264,256]{1,0:T(8,128)(2,1)S(1)}, u32[]{:S(2)}, u32[]{:S(2)}) collective-permute-start(bf16[264,256]{1,0:T(8,128)(2,1)S(1)} %collective-permute-done.refs_1_), channel_id=1, source_target_pairs={{0,4},{1,5},{2,6},{3,7},{4,8},{5,9},{6,10},{7,11},{8,12},{9,13},{1... | collective-permute-start | bytes 405512 | tf_op jit(solution)/shard_map/ppermute | solution.py:40
  66.2 10.9 %collective-permute-start.2 = (bf16[264,256]{1,0:T(8,128)(2,1)S(1)}, bf16[264,256]{1,0:T(8,128)(2,1)S(1)}, u32[]{:S(2)}, u32[]{:S(2)}) collective-permute-start(bf16[264,256]{1,0:T(8,128)(2,1)S(1)} %collective-permute-done.refs_1_), channel_id=1, source_target_pairs={{0,2},{1,3},{2,4},{3,5},{4,6},{5,7},{6,8},{7,9},{8,10},{9,11},{10,... | collective-permute-start | bytes 405512 | tf_op jit(solution)/shard_map/ppermute | solution.py:40
  69.2 0.7 copy-start.2
  84.4 45.3 %collective-permute-start.11 = (bf16[512,512]{1,0:T(8,128)(2,1)S(1)}, bf16[512,512]{1,0:T(8,128)(2,1)S(1)}, u32[]{:S(2)}, u32[]{:S(2)}) collective-permute-start(bf16[512,512]{1,0:T(8,128)(2,1)S(1)} %get-tuple-element.33), channel_id=1, source_target_pairs={{6,0},{7,1},{8,2},{9,3},{10,4},{11,5},{12,6},{13,7},{14,8},{15,9},... | collective-permute-start | bytes 1572872 | tf_op jit(solution)/shard_map/ppermute | solution.py:40
  88.9 40.8 %collective-permute-start.12 = (bf16[512,512]{1,0:T(8,128)(2,1)S(1)}, bf16[512,512]{1,0:T(8,128)(2,1)}, u32[]{:S(2)}, u32[]{:S(2)}) collective-permute-start(bf16[512,512]{1,0:T(8,128)(2,1)S(1)} %get-tuple-element.34), channel_id=1, source_target_pairs={{4,0},{5,1},{6,2},{7,3},{8,4},{9,5},{10,6},{11,7},{12,8},{13,9},{1... | collective-permute-start | bytes 1572872 | tf_op jit(solution)/shard_map/ppermute | solution.py:40
  94.7 35.0 %collective-permute-start.13 = (bf16[512,512]{1,0:T(8,128)(2,1)S(1)}, bf16[512,512]{1,0:T(8,128)(2,1)}, u32[]{:S(2)}, u32[]{:S(2)}) collective-permute-start(bf16[512,512]{1,0:T(8,128)(2,1)S(1)} %get-tuple-element.35), channel_id=1, source_target_pairs={{2,0},{3,1},{4,2},{5,3},{6,4},{7,5},{8,6},{9,7},{10,8},{11,9},{12,... | collective-permute-start | bytes 1572872 | tf_op jit(solution)/shard_map/ppermute | solution.py:40
  120.3 17.3 %all-to-all-start.1 = ((f32[64,1,128]{2,1,0:T(1,128)}), f32[64,1,128]{2,1,0:T(1,128)S(1)}, u32[]{:S(2)}, u32[]{:S(2)}) async-start(f32[64,1,128]{2,1,0:T(1,128)} %broadcast_in_dim.38), calls=%async_computation.1 | async-start | bytes 65536 | tf_op jit(solution)/shard_map/all_to_all | solution.py:231
  131.2 36.4 %collective-permute-start.14 = (bf16[256,512]{1,0:T(8,128)(2,1)S(1)}, bf16[256,512]{1,0:T(8,128)(2,1)S(1)}, u32[]{:S(2)}, u32[]{:S(2)}) collective-permute-start(bf16[256,512]{1,0:T(8,128)(2,1)S(1)} %slice.73), channel_id=1, source_target_pairs={{1,0},{2,1},{3,2},{4,3},{5,4},{6,5},{7,6},{8,7},{9,8},{10,9},{11,1... | collective-permute-start | bytes 786440 | tf_op jit(solution)/shard_map/ppermute | solution.py:40
